TPU v7x, 32 devices: a whole 2x2x4 slice. The times are simulated.
32 devices in a mesh: seq: 8 (over z, x), head: 4 (over y, core).
Axes of the slice: x: 2, y: 2, z: 4, core: 2. Of those that a mesh axis runs over, the one named last changes fastest.
Arguments:
- queries: bfloat16 [2048, 64, 128], P('seq', 'head'), may hold values from -8 to 8
- key_vectors: bfloat16 [2048, 8, 128], P('seq', 'head'), may hold values from -8 to 8
- values: bfloat16 [2048, 8, 128], P('seq', 'head'), may hold values from -6 to 6
- grad_out: bfloat16 [2048, 64, 128], P('seq', 'head'), may hold values from -6 to 6
- key_blocks: int32 [16, 8], P('seq'), may hold values from -1 to 15, as said below
Outputs:
- grad_query: bfloat16 [8192, 2048], P(('head', 'seq'))
- grad_key: bfloat16 [1024, 2048], P(('head', 'seq'))
- grad_value: bfloat16 [1024, 2048], P(('head', 'seq'))
Inputs may be any that keep to these rules, and one draw needn't show every extreme that they name: `key_blocks`: row b belongs to query block b, whose position is p_b. Each row holds p_b once; its other entries are distinct positions from p_b - 6 to p_b - 1, position 0, or -1 for unused; the order within a row is arbitrary.
All inputs are finite; a program needn't handle non-finite values.
Results may differ from a plain program's by a relative error of at most 0.0153.
Values may be sent and summed in bfloat16 or wider, within the bound.
A program may use at most 64 MiB of HBM per device.

v0:
```python
import math

import jax
import jax.numpy as jnp
from jax import lax
from jax.sharding import PartitionSpec as P


def padded(array, sides, width):
    for axis, dim in sides:
        devices, length = (lax.axis_size(axis), array.shape[dim])
        up = [(i, (i + 1) % devices) for i in range(devices - 1)]
        down = [(j, i) for i, j in up]
        last = lax.slice_in_dim(array, length - width, length, axis=dim)
        leading = lax.slice_in_dim(array, 0, width, axis=dim)
        before = lax.ppermute(last, axis, up)
        after = lax.ppermute(leading, axis, down)
        array = jnp.concatenate([before, array, after], axis=dim)
    return array


def from_root(array, axis, root):
    mine = lax.axis_index(axis) == root
    return lax.psum(jnp.where(mine, array, jnp.zeros_like(array)), axis)


def per_device(queries, key_vectors, values, grad_out, key_blocks):
    seq_count = lax.axis_size("seq")
    seq_index = lax.axis_index("seq")
    block_len = queries.shape[0] // 2
    kv_heads = key_vectors.shape[1]
    group_size = queries.shape[1] // kv_heads
    head_dim = queries.shape[2]
    window = key_blocks.shape[1] - 2
    softmax_scale = 1.0 / math.sqrt(head_dim)
    query_pair = queries.reshape(2, block_len, kv_heads, group_size, head_dim)
    grad_pair = grad_out.reshape(2, block_len, kv_heads, group_size, head_dim)
    own_pair = jnp.stack(
        [
            key_vectors.reshape(2, block_len, kv_heads, head_dim),
            values.reshape(2, block_len, kv_heads, head_dim),
        ],
        axis=1,
    )
    positions = jnp.stack([seq_index, 2 * seq_count - 1 - seq_index])
    at_end = seq_index == seq_count - 1
    offsets = jnp.arange(window + 1, dtype=jnp.int32)
    wanted = positions[None, :] - offsets[:, None]
    window_hits = jnp.any(key_blocks[None, :, :] == wanted[:, :, None], axis=2) & (wanted >= 0)
    sink_hits = jnp.any(key_blocks == 0, axis=1) & (positions > window)
    listed = jnp.concatenate([window_hits[:1], sink_hits[None], window_hits[1:]], axis=0)

    def step_down(chain_state, ignored):
        extended = padded(chain_state, (("seq", 0),), 1)
        lower_slot = extended[0]
        upper_slot = jnp.where(at_end, chain_state[1], extended[3])
        return (jnp.stack([upper_slot, lower_slot]), jnp.stack([lower_slot, upper_slot]))

    ignored_state, chain_pairs = lax.scan(step_down, own_pair[::-1], None, length=window)
    sink_pair = from_root(own_pair[0], "seq", 0)
    candidates = jnp.concatenate(
        [
            own_pair[None],
            jnp.broadcast_to(sink_pair[None, None], (1, 2) + sink_pair.shape),
            chain_pairs,
        ],
        axis=0,
    )
    is_self = jnp.arange(window + 2) == 0
    token_index = jnp.arange(block_len)
    causal = token_index[None, :] <= token_index[:, None]

    def allowed_pairs(listed_here, is_first):
        return (
            listed_here[:, None, None, None, None]
            & (causal | jnp.logical_not(is_first))[None, None, None]
        )

    def scores_of(query_side, key_side):
        return (
            jnp.einsum(
                "aihgd,athd->ahgit", query_side, key_side, preferred_element_type=jnp.float32
            )
            * softmax_scale
        )

    def probs_of(query_side, key_side, allowed, norm_rows):
        return jnp.where(
            allowed, jnp.exp(scores_of(query_side, key_side) - norm_rows[..., None]), 0.0
        )

    stats_shape = (2, kv_heads, group_size, block_len)

    def stats_step(running, block_item):
        key_value, listed_here, is_first = block_item
        row_max, row_sum = running
        allowed = allowed_pairs(listed_here, is_first)
        scores = scores_of(query_pair, key_value[:, 0])
        new_max = jnp.maximum(row_max, jnp.max(jnp.where(allowed, scores, -jnp.inf), axis=-1))
        new_sum = row_sum * jnp.exp(row_max - new_max) + jnp.sum(
            jnp.where(allowed, jnp.exp(scores - new_max[..., None]), 0.0), axis=-1
        )
        return ((new_max, new_sum), None)

    block_items = (candidates, listed, is_self)
    row_max, row_sum = lax.scan(
        stats_step,
        (jnp.full(stats_shape, -jnp.inf, jnp.float32), jnp.zeros(stats_shape, jnp.float32)),
        block_items,
    )[0]
    log_norm = row_max + jnp.log(row_sum)

    def output_step(totals, block_item):
        key_value, listed_here, is_first = block_item
        attn_probs = probs_of(
            query_pair, key_value[:, 0], allowed_pairs(listed_here, is_first), log_norm
        )
        return (
            totals
            + jnp.einsum(
                "ahgit,athd->aihgd",
                attn_probs.astype(jnp.bfloat16),
                key_value[:, 1],
                preferred_element_type=jnp.float32,
            ),
            None,
        )

    attn_out = lax.scan(output_step, jnp.zeros(query_pair.shape, jnp.float32), block_items)[0]
    row_delta = jnp.einsum(
        "aihgd,aihgd->ahgi", grad_pair, attn_out, preferred_element_type=jnp.float32
    )

    def key_terms(query_side, grad_side, key_value, allowed, norm_rows, delta_rows):
        attn_probs = probs_of(query_side, key_value[:, 0], allowed, norm_rows)
        grad_probs = jnp.einsum(
            "aihgd,athd->ahgit", grad_side, key_value[:, 1], preferred_element_type=jnp.float32
        )
        grad_scores = (attn_probs * (grad_probs - delta_rows[..., None])).astype(jnp.bfloat16)
        return (attn_probs.astype(jnp.bfloat16), grad_scores)

    def key_grads(query_side, grad_side, attn_low, grad_scores):
        grad_key = (
            jnp.einsum(
                "ahgit,aihgd->hdat", grad_scores, query_side, preferred_element_type=jnp.float32
            )
            * softmax_scale
        )
        grad_value = jnp.einsum(
            "ahgit,aihgd->hdat", attn_low, grad_side, preferred_element_type=jnp.float32
        )
        return jnp.stack([grad_key, grad_value])

    key_zero = jnp.zeros((2, kv_heads, head_dim, 2, block_len), jnp.float32)
    query_zero = jnp.zeros((kv_heads, group_size, head_dim, 2, block_len), jnp.float32)

    def query_step():

        def advance(totals, block_item):
            key_value, listed_here, is_first = block_item
            attn_low, grad_scores = key_terms(
                query_pair,
                grad_pair,
                key_value,
                allowed_pairs(listed_here, is_first),
                log_norm,
                row_delta,
            )
            new_totals = totals + jnp.einsum(
                "ahgit,athd->hgdai",
                grad_scores,
                key_value[:, 0],
                preferred_element_type=jnp.float32,
            )
            return (new_totals, key_grads(query_pair, grad_pair, attn_low, grad_scores))

        return advance

    query_total, key_parts = lax.scan(query_step(), query_zero, block_items)

    def climb_back(running, block_item):
        moving = running + block_item
        extended = padded(moving.astype(jnp.bfloat16), (("seq", 3),), 1).astype(moving.dtype)
        lower_slot = jnp.where(at_end, moving[:, :, :, 1], extended[:, :, :, 3])
        return (jnp.stack([lower_slot, extended[:, :, :, 0]], axis=3), None)

    returned = lax.scan(climb_back, key_zero, key_parts[2:], reverse=True)[0]
    sink_total = lax.psum(jnp.sum(key_parts[1], axis=3), "seq")
    sink_slot = jnp.stack(
        [jnp.where(seq_index == 0, sink_total, 0.0), jnp.zeros_like(sink_total)], axis=3
    )
    key_total = key_parts[0] + returned + sink_slot
    key_rows = key_total.astype(jnp.bfloat16).reshape(2, kv_heads * head_dim, 2 * block_len)
    query_rows = (
        (query_total * softmax_scale)
        .astype(jnp.bfloat16)
        .reshape(1, kv_heads * group_size * head_dim, 2 * block_len)
    )
    query_moved, key_moved = (
        lax.all_to_all(query_rows, "seq", split_axis=1, concat_axis=2, tiled=True),
        lax.all_to_all(key_rows, "seq", split_axis=1, concat_axis=2, tiled=True),
    )
    return (query_moved[0], key_moved[0], key_moved[1])


def solution(mesh):
    return jax.shard_map(
        per_device,
        mesh=mesh,
        in_specs=(
            P("seq", "head", None),
            P("seq", "head", None),
            P("seq", "head", None),
            P("seq", "head", None),
            P("seq", None),
        ),
        out_specs=(P(("head", "seq"), None), P(("head", "seq"), None), P(("head", "seq"), None)),
        check_vma=False,
    )
```

profile of v0, /device:TPU:0, one launch (start us, length us, event | category | flops | bytes accessed | tf_op | source)
XLA Modules:
  0.0 467.5 jit_solution(17782732227160274916)
XLA Ops:
  15.7 98.9 %while.63 = (s32[]{:T(128)}, bf16[2,2,128,2,128]{4,3,2,1,0:T(2,128)(2,1)S(1)}, bf16[6,2,2,128,2,128]{5,3,4,1,2,0:T(8,128)(2,1)}, pred[]{:T(512)}, s32[]{:T(128)}) while((s32[]{:T(128)}, bf16[2,2,128,2,128]{4,3,2,1,0:T(2,128)(2,1)S(1)}, bf16[6,2,2,128,2,128]{5,3,4,1,2,0:T(8,128)(2,1)}, pred[]{:T(512)}, s32[]{:T(128)}) %tuple.149), condition=%wide.region_2.3_spmd, body=%wide.region_1.0_spmd.sunk | while | flops 327682 | bytes 3145882 | solution.py:59
  17.1 7.6 %collective-permute-done = bf16[1,2,128,2,128]{4,3,2,1,0:T(2,128)(2,1)S(1)} collective-permute-done((bf16[1,2,128,2,128]{4,3,2,1,0:T(2,128)(2,1)S(1)}, bf16[1,2,128,2,128]{4,3,2,1,0:T(2,128)(2,1)S(1)}, u32[]{:S(2)}, u32[]{:S(2)}) %collective-permute-start) | collective-permute-done | bytes 131104 | tf_op jit(solution)/shard_map/while/body/eval_jaxpr/ppermute | solution.py:17
  24.9 4.4 collective-permute-start.1
  34.5 6.0 %collective-permute-done = bf16[1,2,128,2,128]{4,3,2,1,0:T(2,128)(2,1)S(1)} collective-permute-done((bf16[1,2,128,2,128]{4,3,2,1,0:T(2,128)(2,1)S(1)}, bf16[1,2,128,2,128]{4,3,2,1,0:T(2,128)(2,1)S(1)}, u32[]{:S(2)}, u32[]{:S(2)}) %collective-permute-start) | collective-permute-done | bytes 131104 | tf_op jit(solution)/shard_map/while/body/eval_jaxpr/ppermute | solution.py:17
  40.7 4.8 %collective-permute-start.1 = (bf16[1,2,128,2,128]{4,3,2,1,0:T(2,128)(2,1)S(1)}, bf16[1,2,128,2,128]{4,3,2,1,0:T(2,128)(2,1)S(1)}, u32[]{:S(2)}, u32[]{:S(2)}) collective-permute-start(bf16[1,2,128,2,128]{4,3,2,1,0:T(2,128)(2,1)S(1)} %get-tuple-element.767), channel_id=1, source_target_pairs={{0,4},{4,8},{8,12},{12,16},{16,20},{20,24},{24,28},{1,5},{5,9},{9,... | collective-permute-start | bytes 393224 | tf_op jit(solution)/shard_map/while/body/eval_jaxpr/ppermute | solution.py:16
  50.6 6.1 %collective-permute-done = bf16[1,2,128,2,128]{4,3,2,1,0:T(2,128)(2,1)S(1)} collective-permute-done((bf16[1,2,128,2,128]{4,3,2,1,0:T(2,128)(2,1)S(1)}, bf16[1,2,128,2,128]{4,3,2,1,0:T(2,128)(2,1)S(1)}, u32[]{:S(2)}, u32[]{:S(2)}) %collective-permute-start) | collective-permute-done | bytes 131104 | tf_op jit(solution)/shard_map/while/body/eval_jaxpr/ppermute | solution.py:17
  56.9 4.8 %collective-permute-start.1 = (bf16[1,2,128,2,128]{4,3,2,1,0:T(2,128)(2,1)S(1)}, bf16[1,2,128,2,128]{4,3,2,1,0:T(2,128)(2,1)S(1)}, u32[]{:S(2)}, u32[]{:S(2)}) collective-permute-start(bf16[1,2,128,2,128]{4,3,2,1,0:T(2,128)(2,1)S(1)} %get-tuple-element.767), channel_id=1, source_target_pairs={{0,4},{4,8},{8,12},{12,16},{16,20},{20,24},{24,28},{1,5},{5,9},{9,... | collective-permute-start | bytes 393224 | tf_op jit(solution)/shard_map/while/body/eval_jaxpr/ppermute | solution.py:16
  66.9 6.0 %collective-permute-done = bf16[1,2,128,2,128]{4,3,2,1,0:T(2,128)(2,1)S(1)} collective-permute-done((bf16[1,2,128,2,128]{4,3,2,1,0:T(2,128)(2,1)S(1)}, bf16[1,2,128,2,128]{4,3,2,1,0:T(2,128)(2,1)S(1)}, u32[]{:S(2)}, u32[]{:S(2)}) %collective-permute-start) | collective-permute-done | bytes 131104 | tf_op jit(solution)/shard_map/while/body/eval_jaxpr/ppermute | solution.py:17
  73.1 4.9 %collective-permute-start.1 = (bf16[1,2,128,2,128]{4,3,2,1,0:T(2,128)(2,1)S(1)}, bf16[1,2,128,2,128]{4,3,2,1,0:T(2,128)(2,1)S(1)}, u32[]{:S(2)}, u32[]{:S(2)}) collective-permute-start(bf16[1,2,128,2,128]{4,3,2,1,0:T(2,128)(2,1)S(1)} %get-tuple-element.767), channel_id=1, source_target_pairs={{0,4},{4,8},{8,12},{12,16},{16,20},{20,24},{24,28},{1,5},{5,9},{9,... | collective-permute-start | bytes 393224 | tf_op jit(solution)/shard_map/while/body/eval_jaxpr/ppermute | solution.py:16
  83.1 6.0 %collective-permute-done = bf16[1,2,128,2,128]{4,3,2,1,0:T(2,128)(2,1)S(1)} collective-permute-done((bf16[1,2,128,2,128]{4,3,2,1,0:T(2,128)(2,1)S(1)}, bf16[1,2,128,2,128]{4,3,2,1,0:T(2,128)(2,1)S(1)}, u32[]{:S(2)}, u32[]{:S(2)}) %collective-permute-start) | collective-permute-done | bytes 131104 | tf_op jit(solution)/shard_map/while/body/eval_jaxpr/ppermute | solution.py:17
  89.3 4.9 %collective-permute-start.1 = (bf16[1,2,128,2,128]{4,3,2,1,0:T(2,128)(2,1)S(1)}, bf16[1,2,128,2,128]{4,3,2,1,0:T(2,128)(2,1)S(1)}, u32[]{:S(2)}, u32[]{:S(2)}) collective-permute-start(bf16[1,2,128,2,128]{4,3,2,1,0:T(2,128)(2,1)S(1)} %get-tuple-element.767), channel_id=1, source_target_pairs={{0,4},{4,8},{8,12},{12,16},{16,20},{20,24},{24,28},{1,5},{5,9},{9,... | collective-permute-start | bytes 393224 | tf_op jit(solution)/shard_map/while/body/eval_jaxpr/ppermute | solution.py:16
  99.3 6.1 %collective-permute-done = bf16[1,2,128,2,128]{4,3,2,1,0:T(2,128)(2,1)S(1)} collective-permute-done((bf16[1,2,128,2,128]{4,3,2,1,0:T(2,128)(2,1)S(1)}, bf16[1,2,128,2,128]{4,3,2,1,0:T(2,128)(2,1)S(1)}, u32[]{:S(2)}, u32[]{:S(2)}) %collective-permute-start) | collective-permute-done | bytes 131104 | tf_op jit(solution)/shard_map/while/body/eval_jaxpr/ppermute | solution.py:17
  105.6 5.3 %collective-permute-start.1 = (bf16[1,2,128,2,128]{4,3,2,1,0:T(2,128)(2,1)S(1)}, bf16[1,2,128,2,128]{4,3,2,1,0:T(2,128)(2,1)S(1)}, u32[]{:S(2)}, u32[]{:S(2)}) collective-permute-start(bf16[1,2,128,2,128]{4,3,2,1,0:T(2,128)(2,1)S(1)} %get-tuple-element.767), channel_id=1, source_target_pairs={{0,4},{4,8},{8,12},{12,16},{16,20},{20,24},{24,28},{1,5},{5,9},{9,... | collective-permute-start | bytes 393224 | tf_op jit(solution)/shard_map/while/body/eval_jaxpr/ppermute | solution.py:16
  118.6 27.0 %while.65 = (s32[]{:T(128)}, f32[2,2,8,128]{3,2,1,0:T(8,128)S(1)}, f32[2,2,8,128]{3,2,1,0:T(8,128)S(1)}, pred[8,2]{1,0:T(8,128)(4,1)S(1)}, pred[8]{0:T(512)(128)...) while((s32[]{:T(128)}, f32[2,2,8,128]{3,2,1,0:T(8,128)S(1)}, ...), condition=%wide.region_8.9_spmd.clone, body=%wide.region_5.8_spmd.clone.sunk | while | flops 137973760 | bytes 6242431 | solution.py:106
  145.6 47.2 %while.66 = (s32[]{:T(128)}, f32[2,128,2,8,128]{1,4,3,2,0:T(8,128)}, bf16[8,2,2,128,2,128]{5,3,4,1,2,0:T(8,128)(2,1)}, pred[8,2]{1,0:T(8,128)(4,1)S(1)}, pred[8]...) while((s32[]{:T(128)}, ...), condition=%wide.region_10.11_spmd.clone, body=%wide.region_9.10_spmd.clone.sunk | while | flops 271646720 | bytes 6144126 | solution.py:129
  158.6 3.7 bitcast_add_fusion.7
  198.5 69.3 %while.67 = (s32[]{:T(128)}, f32[2,8,128,2,128]{4,2,1,3,0:T(8,128)S(1)}, f32[8,2,2,128,2,128]{3,5,4,2,1,0:T(8,128)}, bf16[8,2,2,128,2,128]{5,3,4,1,2,0:T(8,128)(...) while((s32[]{:T(128)}, ...), condition=%wide.region_12.13_spmd.clone, body=%wide.region_11.12_spmd.clone.sunk | while | flops 676069376 | bytes 24642224 | solution.py:179
  267.9 3.9 slice.98
  274.6 133.2 %while.64 = (s32[]{:T(128)}, f32[2,2,128,2,128]{4,3,2,1,0:T(2,128)}, pred[]{:T(512)}, f32[6,2,2,128,2,128]{3,5,4,2,1,0:T(8,128)}, s32[]{:T(128)}, /*index=5*/s32[]{:T(128)}) while((s32[]{:T(128)}, f32[2,2,128,2,128]{4,3,2,1,0:T(2,128)}, pred[]{:T(512)}, f32[6,2,2,128,2,128]{3,5,4,2,1,0:T(8,128)}, s32[]{:T(128)}, ...), condition=%wide.region_14.15_spmd, body=%wide.region_13.14_spmd.sunk | while | flops 1245187 | bytes 10485954 | solution.py:187
  282.4 5.0 %collective-permute-start.3 = (bf16[2,2,128,1,128]{4,3,2,1,0:T(2,128)(2,1)}, bf16[2,2,128,1,128]{4,3,2,1,0:T(2,128)(2,1)S(1)}, u32[]{:S(2)}, u32[]{:S(2)}) collective-permute-start(bf16[2,2,128,1,128]{4,3,2,1,0:T(2,128)(2,1)} %get-tuple-element.776), channel_id=1, source_target_pairs={{0,4},{4,8},{8,12},{12,16},{16,20},{20,24},{24,28},{1,5},{5,9},{9,... | collective-permute-start | bytes 393224 | tf_op jit(solution)/shard_map/while/body/eval_jaxpr/ppermute | solution.py:16
  290.0 4.0 collective-permute-done.3
  304.9 4.9 %collective-permute-start.3 = (bf16[2,2,128,1,128]{4,3,2,1,0:T(2,128)(2,1)}, bf16[2,2,128,1,128]{4,3,2,1,0:T(2,128)(2,1)S(1)}, u32[]{:S(2)}, u32[]{:S(2)}) collective-permute-start(bf16[2,2,128,1,128]{4,3,2,1,0:T(2,128)(2,1)} %get-tuple-element.776), channel_id=1, source_target_pairs={{0,4},{4,8},{8,12},{12,16},{16,20},{20,24},{24,28},{1,5},{5,9},{9,... | collective-permute-start | bytes 393224 | tf_op jit(solution)/shard_map/while/body/eval_jaxpr/ppermute | solution.py:16
  326.7 4.9 %collective-permute-start.3 = (bf16[2,2,128,1,128]{4,3,2,1,0:T(2,128)(2,1)}, bf16[2,2,128,1,128]{4,3,2,1,0:T(2,128)(2,1)S(1)}, u32[]{:S(2)}, u32[]{:S(2)}) collective-permute-start(bf16[2,2,128,1,128]{4,3,2,1,0:T(2,128)(2,1)} %get-tuple-element.776), channel_id=1, source_target_pairs={{0,4},{4,8},{8,12},{12,16},{16,20},{20,24},{24,28},{1,5},{5,9},{9,... | collective-permute-start | bytes 393224 | tf_op jit(solution)/shard_map/while/body/eval_jaxpr/ppermute | solution.py:16
  334.2 4.3 collective-permute-done.3
  349.4 4.9 %collective-permute-start.3 = (bf16[2,2,128,1,128]{4,3,2,1,0:T(2,128)(2,1)}, bf16[2,2,128,1,128]{4,3,2,1,0:T(2,128)(2,1)S(1)}, u32[]{:S(2)}, u32[]{:S(2)}) collective-permute-start(bf16[2,2,128,1,128]{4,3,2,1,0:T(2,128)(2,1)} %get-tuple-element.776), channel_id=1, source_target_pairs={{0,4},{4,8},{8,12},{12,16},{16,20},{20,24},{24,28},{1,5},{5,9},{9,... | collective-permute-start | bytes 393224 | tf_op jit(solution)/shard_map/while/body/eval_jaxpr/ppermute | solution.py:16
  371.2 4.9 %collective-permute-start.3 = (bf16[2,2,128,1,128]{4,3,2,1,0:T(2,128)(2,1)}, bf16[2,2,128,1,128]{4,3,2,1,0:T(2,128)(2,1)S(1)}, u32[]{:S(2)}, u32[]{:S(2)}) collective-permute-start(bf16[2,2,128,1,128]{4,3,2,1,0:T(2,128)(2,1)} %get-tuple-element.776), channel_id=1, source_target_pairs={{0,4},{4,8},{8,12},{12,16},{16,20},{20,24},{24,28},{1,5},{5,9},{9,... | collective-permute-start | bytes 393224 | tf_op jit(solution)/shard_map/while/body/eval_jaxpr/ppermute | solution.py:16
  393.0 4.9 %collective-permute-start.3 = (bf16[2,2,128,1,128]{4,3,2,1,0:T(2,128)(2,1)}, bf16[2,2,128,1,128]{4,3,2,1,0:T(2,128)(2,1)S(1)}, u32[]{:S(2)}, u32[]{:S(2)}) collective-permute-start(bf16[2,2,128,1,128]{4,3,2,1,0:T(2,128)(2,1)} %get-tuple-element.776), channel_id=1, source_target_pairs={{0,4},{4,8},{8,12},{12,16},{16,20},{20,24},{24,28},{1,5},{5,9},{9,... | collective-permute-start | bytes 393224 | tf_op jit(solution)/shard_map/while/body/eval_jaxpr/ppermute | solution.py:16
  400.5 4.1 collective-permute-done.3
  412.2 8.8 %all-to-all-start.1 = ((bf16[2,256,256]{2,0,1:T(2,128)(2,1)}), bf16[2,256,256]{2,0,1:T(2,128)(2,1)S(1)}, u32[]{:S(2)}, u32[]{:S(2)}) async-start(bf16[2,256,256]{2,0,1:T(2,128)(2,1)} %reshape.142), calls=%async_computation.1 | async-start | bytes 524288 | tf_op jit(solution)/shard_map/all_to_all | solution.py:201
  423.3 10.6 %reduce.3 = bf16[2048,256]{1,0:T(8,128)(2,1)S(1)} reduce(bf16[2048,1,256]{2,1,0:T(2,128)(2,1)S(1)} %bitcast.230, bf16[]{:T(256)} %broadcast.163), dimensions={1}, to_apply=%bitcast.154.reduce_sub_computation | reduce | bytes 2097154
  435.1 6.0 %all-to-all-start = ((bf16[8,2,32768]{2,1,0:T(2,128)(2,1)}), bf16[8,2,32768]{2,1,0:T(2,128)(2,1)S(1)}, u32[]{:S(2)}, u32[]{:S(2)}) async-start(bf16[8,2,32768]{2,1,0:T(2,128)(2,1)} %reshape.143), calls=%async_computation | async-start | bytes 2097152 | tf_op jit(solution)/shard_map/all_to_all | solution.py:200
  442.4 15.0 %all-to-all-done = bf16[8,2,32768]{2,1,0:T(2,128)(2,1)S(1)} async-done(((bf16[8,2,32768]{2,1,0:T(2,128)(2,1)}), bf16[8,2,32768]{2,1,0:T(2,128)(2,1)S(1)}, u32[]{:S(2)}, u32[]{:S(2)}) %all-to-all-start) | async-done | bytes 1048608 | tf_op jit(solution)/shard_map/all_to_all | solution.py:200
  (405 shorter events, 278.6 us)
Async XLA Ops:
  7.2 107.5 %all-reduce.4.cloned.1.call-start = ((), (), s32[]{:S(2)}) async-start(), calls=%async_computation.2 | async-start | bytes 262144 | tf_op jit(solution)/shard_map/psum | solution.py:24
  9.9 399.1 %all-reduce.6.cloned.1.call-start = ((), (), s32[]{:S(2)}) async-start(), calls=%async_computation.3 | async-start | bytes 524288 | tf_op jit(solution)/shard_map/psum | solution.py:188
  15.8 8.9 %collective-permute-start = (bf16[1,2,128,2,128]{4,3,2,1,0:T(2,128)(2,1)S(1)}, bf16[1,2,128,2,128]{4,3,2,1,0:T(2,128)(2,1)S(1)}, u32[]{:S(2)}, u32[]{:S(2)}) collective-permute-start(bf16[1,2,128,2,128]{4,3,2,1,0:T(2,128)(2,1)S(1)} %slice.170), channel_id=1, source_target_pairs={{4,0},{8,4},{12,8},{16,12},{20,16},{24,20},{28,24},{5,1},{9,5},{13... | collective-permute-start | bytes 393224 | tf_op jit(solution)/shard_map/while/body/eval_jaxpr/ppermute | solution.py:17
  24.9 6.9 %collective-permute-start.1 = (bf16[1,2,128,2,128]{4,3,2,1,0:T(2,128)(2,1)S(1)}, bf16[1,2,128,2,128]{4,3,2,1,0:T(2,128)(2,1)S(1)}, u32[]{:S(2)}, u32[]{:S(2)}) collective-permute-start(bf16[1,2,128,2,128]{4,3,2,1,0:T(2,128)(2,1)S(1)} %get-tuple-element.767), channel_id=1, source_target_pairs={{0,4},{4,8},{8,12},{12,16},{16,20},{20,24},{24,28},{1,5},{5,9},{9,... | collective-permute-start | bytes 393224 | tf_op jit(solution)/shard_map/while/body/eval_jaxpr/ppermute | solution.py:16
  33.2 7.3 %collective-permute-start = (bf16[1,2,128,2,128]{4,3,2,1,0:T(2,128)(2,1)S(1)}, bf16[1,2,128,2,128]{4,3,2,1,0:T(2,128)(2,1)S(1)}, u32[]{:S(2)}, u32[]{:S(2)}) collective-permute-start(bf16[1,2,128,2,128]{4,3,2,1,0:T(2,128)(2,1)S(1)} %slice.170), channel_id=1, source_target_pairs={{4,0},{8,4},{12,8},{16,12},{20,16},{24,20},{28,24},{5,1},{9,5},{13... | collective-permute-start | bytes 393224 | tf_op jit(solution)/shard_map/while/body/eval_jaxpr/ppermute | solution.py:17
  40.7 7.3 %collective-permute-start.1 = (bf16[1,2,128,2,128]{4,3,2,1,0:T(2,128)(2,1)S(1)}, bf16[1,2,128,2,128]{4,3,2,1,0:T(2,128)(2,1)S(1)}, u32[]{:S(2)}, u32[]{:S(2)}) collective-permute-start(bf16[1,2,128,2,128]{4,3,2,1,0:T(2,128)(2,1)S(1)} %get-tuple-element.767), channel_id=1, source_target_pairs={{0,4},{4,8},{8,12},{12,16},{16,20},{20,24},{24,28},{1,5},{5,9},{9,... | collective-permute-start | bytes 393224 | tf_op jit(solution)/shard_map/while/body/eval_jaxpr/ppermute | solution.py:16
  49.3 7.4 %collective-permute-start = (bf16[1,2,128,2,128]{4,3,2,1,0:T(2,128)(2,1)S(1)}, bf16[1,2,128,2,128]{4,3,2,1,0:T(2,128)(2,1)S(1)}, u32[]{:S(2)}, u32[]{:S(2)}) collective-permute-start(bf16[1,2,128,2,128]{4,3,2,1,0:T(2,128)(2,1)S(1)} %slice.170), channel_id=1, source_target_pairs={{4,0},{8,4},{12,8},{16,12},{20,16},{24,20},{28,24},{5,1},{9,5},{13... | collective-permute-start | bytes 393224 | tf_op jit(solution)/shard_map/while/body/eval_jaxpr/ppermute | solution.py:17
  56.9 7.3 %collective-permute-start.1 = (bf16[1,2,128,2,128]{4,3,2,1,0:T(2,128)(2,1)S(1)}, bf16[1,2,128,2,128]{4,3,2,1,0:T(2,128)(2,1)S(1)}, u32[]{:S(2)}, u32[]{:S(2)}) collective-permute-start(bf16[1,2,128,2,128]{4,3,2,1,0:T(2,128)(2,1)S(1)} %get-tuple-element.767), channel_id=1, source_target_pairs={{0,4},{4,8},{8,12},{12,16},{16,20},{20,24},{24,28},{1,5},{5,9},{9,... | collective-permute-start | bytes 393224 | tf_op jit(solution)/shard_map/while/body/eval_jaxpr/ppermute | solution.py:16
  65.6 7.3 %collective-permute-start = (bf16[1,2,128,2,128]{4,3,2,1,0:T(2,128)(2,1)S(1)}, bf16[1,2,128,2,128]{4,3,2,1,0:T(2,128)(2,1)S(1)}, u32[]{:S(2)}, u32[]{:S(2)}) collective-permute-start(bf16[1,2,128,2,128]{4,3,2,1,0:T(2,128)(2,1)S(1)} %slice.170), channel_id=1, source_target_pairs={{4,0},{8,4},{12,8},{16,12},{20,16},{24,20},{28,24},{5,1},{9,5},{13... | collective-permute-start | bytes 393224 | tf_op jit(solution)/shard_map/while/body/eval_jaxpr/ppermute | solution.py:17
  73.1 7.4 %collective-permute-start.1 = (bf16[1,2,128,2,128]{4,3,2,1,0:T(2,128)(2,1)S(1)}, bf16[1,2,128,2,128]{4,3,2,1,0:T(2,128)(2,1)S(1)}, u32[]{:S(2)}, u32[]{:S(2)}) collective-permute-start(bf16[1,2,128,2,128]{4,3,2,1,0:T(2,128)(2,1)S(1)} %get-tuple-element.767), channel_id=1, source_target_pairs={{0,4},{4,8},{8,12},{12,16},{16,20},{20,24},{24,28},{1,5},{5,9},{9,... | collective-permute-start | bytes 393224 | tf_op jit(solution)/shard_map/while/body/eval_jaxpr/ppermute | solution.py:16
  81.8 7.3 %collective-permute-start = (bf16[1,2,128,2,128]{4,3,2,1,0:T(2,128)(2,1)S(1)}, bf16[1,2,128,2,128]{4,3,2,1,0:T(2,128)(2,1)S(1)}, u32[]{:S(2)}, u32[]{:S(2)}) collective-permute-start(bf16[1,2,128,2,128]{4,3,2,1,0:T(2,128)(2,1)S(1)} %slice.170), channel_id=1, source_target_pairs={{4,0},{8,4},{12,8},{16,12},{20,16},{24,20},{28,24},{5,1},{9,5},{13... | collective-permute-start | bytes 393224 | tf_op jit(solution)/shard_map/while/body/eval_jaxpr/ppermute | solution.py:17
  89.3 7.4 %collective-permute-start.1 = (bf16[1,2,128,2,128]{4,3,2,1,0:T(2,128)(2,1)S(1)}, bf16[1,2,128,2,128]{4,3,2,1,0:T(2,128)(2,1)S(1)}, u32[]{:S(2)}, u32[]{:S(2)}) collective-permute-start(bf16[1,2,128,2,128]{4,3,2,1,0:T(2,128)(2,1)S(1)} %get-tuple-element.767), channel_id=1, source_target_pairs={{0,4},{4,8},{8,12},{12,16},{16,20},{20,24},{24,28},{1,5},{5,9},{9,... | collective-permute-start | bytes 393224 | tf_op jit(solution)/shard_map/while/body/eval_jaxpr/ppermute | solution.py:16
  98.0 7.4 %collective-permute-start = (bf16[1,2,128,2,128]{4,3,2,1,0:T(2,128)(2,1)S(1)}, bf16[1,2,128,2,128]{4,3,2,1,0:T(2,128)(2,1)S(1)}, u32[]{:S(2)}, u32[]{:S(2)}) collective-permute-start(bf16[1,2,128,2,128]{4,3,2,1,0:T(2,128)(2,1)S(1)} %slice.170), channel_id=1, source_target_pairs={{4,0},{8,4},{12,8},{16,12},{20,16},{24,20},{28,24},{5,1},{9,5},{13... | collective-permute-start | bytes 393224 | tf_op jit(solution)/shard_map/while/body/eval_jaxpr/ppermute | solution.py:17
  105.6 7.9 %collective-permute-start.1 = (bf16[1,2,128,2,128]{4,3,2,1,0:T(2,128)(2,1)S(1)}, bf16[1,2,128,2,128]{4,3,2,1,0:T(2,128)(2,1)S(1)}, u32[]{:S(2)}, u32[]{:S(2)}) collective-permute-start(bf16[1,2,128,2,128]{4,3,2,1,0:T(2,128)(2,1)S(1)} %get-tuple-element.767), channel_id=1, source_target_pairs={{0,4},{4,8},{8,12},{12,16},{16,20},{20,24},{24,28},{1,5},{5,9},{9,... | collective-permute-start | bytes 393224 | tf_op jit(solution)/shard_map/while/body/eval_jaxpr/ppermute | solution.py:16
  279.9 14.8 %copy-start.2 = (f32[2,2,128,2,128]{4,3,2,1,0:T(2,128)S(1)}, f32[2,2,128,2,128]{4,3,2,1,0:T(2,128)}, u32[]{:S(2)}) copy-start(f32[2,2,128,2,128]{4,3,2,1,0:T(2,128)} %get-tuple-element.777) | copy-start | bytes 1572868 | tf_op jit(solution)/shard_map/while
  281.1 8.9 %collective-permute-start.2 = (bf16[2,2,128,1,128]{4,3,2,1,0:T(2,128)(2,1)}, bf16[2,2,128,1,128]{4,3,2,1,0:T(2,128)(2,1)S(1)}, u32[]{:S(2)}, u32[]{:S(2)}) collective-permute-start(bf16[2,2,128,1,128]{4,3,2,1,0:T(2,128)(2,1)} %get-tuple-element.775), channel_id=1, source_target_pairs={{4,0},{8,4},{12,8},{16,12},{20,16},{24,20},{28,24},{5,1},{9,5},{13... | collective-permute-start | bytes 393224 | tf_op jit(solution)/shard_map/while/body/eval_jaxpr/ppermute | solution.py:17
  282.4 11.6 %collective-permute-start.3 = (bf16[2,2,128,1,128]{4,3,2,1,0:T(2,128)(2,1)}, bf16[2,2,128,1,128]{4,3,2,1,0:T(2,128)(2,1)S(1)}, u32[]{:S(2)}, u32[]{:S(2)}) collective-permute-start(bf16[2,2,128,1,128]{4,3,2,1,0:T(2,128)(2,1)} %get-tuple-element.776), channel_id=1, source_target_pairs={{0,4},{4,8},{8,12},{12,16},{16,20},{20,24},{24,28},{1,5},{5,9},{9,... | collective-permute-start | bytes 393224 | tf_op jit(solution)/shard_map/while/body/eval_jaxpr/ppermute | solution.py:16
  303.6 8.8 %collective-permute-start.2 = (bf16[2,2,128,1,128]{4,3,2,1,0:T(2,128)(2,1)}, bf16[2,2,128,1,128]{4,3,2,1,0:T(2,128)(2,1)S(1)}, u32[]{:S(2)}, u32[]{:S(2)}) collective-permute-start(bf16[2,2,128,1,128]{4,3,2,1,0:T(2,128)(2,1)} %get-tuple-element.775), channel_id=1, source_target_pairs={{4,0},{8,4},{12,8},{16,12},{20,16},{24,20},{28,24},{5,1},{9,5},{13... | collective-permute-start | bytes 393224 | tf_op jit(solution)/shard_map/while/body/eval_jaxpr/ppermute | solution.py:17
  304.9 10.9 %collective-permute-start.3 = (bf16[2,2,128,1,128]{4,3,2,1,0:T(2,128)(2,1)}, bf16[2,2,128,1,128]{4,3,2,1,0:T(2,128)(2,1)S(1)}, u32[]{:S(2)}, u32[]{:S(2)}) collective-permute-start(bf16[2,2,128,1,128]{4,3,2,1,0:T(2,128)(2,1)} %get-tuple-element.776), channel_id=1, source_target_pairs={{0,4},{4,8},{8,12},{12,16},{16,20},{20,24},{24,28},{1,5},{5,9},{9,... | collective-permute-start | bytes 393224 | tf_op jit(solution)/shard_map/while/body/eval_jaxpr/ppermute | solution.py:16
  324.2 15.1 %copy-start.2 = (f32[2,2,128,2,128]{4,3,2,1,0:T(2,128)S(1)}, f32[2,2,128,2,128]{4,3,2,1,0:T(2,128)}, u32[]{:S(2)}) copy-start(f32[2,2,128,2,128]{4,3,2,1,0:T(2,128)} %get-tuple-element.777) | copy-start | bytes 1572868 | tf_op jit(solution)/shard_map/while
  325.4 8.8 %collective-permute-start.2 = (bf16[2,2,128,1,128]{4,3,2,1,0:T(2,128)(2,1)}, bf16[2,2,128,1,128]{4,3,2,1,0:T(2,128)(2,1)S(1)}, u32[]{:S(2)}, u32[]{:S(2)}) collective-permute-start(bf16[2,2,128,1,128]{4,3,2,1,0:T(2,128)(2,1)} %get-tuple-element.775), channel_id=1, source_target_pairs={{4,0},{8,4},{12,8},{16,12},{20,16},{24,20},{28,24},{5,1},{9,5},{13... | collective-permute-start | bytes 393224 | tf_op jit(solution)/shard_map/while/body/eval_jaxpr/ppermute | solution.py:17
  326.7 11.8 %collective-permute-start.3 = (bf16[2,2,128,1,128]{4,3,2,1,0:T(2,128)(2,1)}, bf16[2,2,128,1,128]{4,3,2,1,0:T(2,128)(2,1)S(1)}, u32[]{:S(2)}, u32[]{:S(2)}) collective-permute-start(bf16[2,2,128,1,128]{4,3,2,1,0:T(2,128)(2,1)} %get-tuple-element.776), channel_id=1, source_target_pairs={{0,4},{4,8},{8,12},{12,16},{16,20},{20,24},{24,28},{1,5},{5,9},{9,... | collective-permute-start | bytes 393224 | tf_op jit(solution)/shard_map/while/body/eval_jaxpr/ppermute | solution.py:16
  348.1 8.8 %collective-permute-start.2 = (bf16[2,2,128,1,128]{4,3,2,1,0:T(2,128)(2,1)}, bf16[2,2,128,1,128]{4,3,2,1,0:T(2,128)(2,1)S(1)}, u32[]{:S(2)}, u32[]{:S(2)}) collective-permute-start(bf16[2,2,128,1,128]{4,3,2,1,0:T(2,128)(2,1)} %get-tuple-element.775), channel_id=1, source_target_pairs={{4,0},{8,4},{12,8},{16,12},{20,16},{24,20},{28,24},{5,1},{9,5},{13... | collective-permute-start | bytes 393224 | tf_op jit(solution)/shard_map/while/body/eval_jaxpr/ppermute | solution.py:17
  349.4 10.9 %collective-permute-start.3 = (bf16[2,2,128,1,128]{4,3,2,1,0:T(2,128)(2,1)}, bf16[2,2,128,1,128]{4,3,2,1,0:T(2,128)(2,1)S(1)}, u32[]{:S(2)}, u32[]{:S(2)}) collective-permute-start(bf16[2,2,128,1,128]{4,3,2,1,0:T(2,128)(2,1)} %get-tuple-element.776), channel_id=1, source_target_pairs={{0,4},{4,8},{8,12},{12,16},{16,20},{20,24},{24,28},{1,5},{5,9},{9,... | collective-permute-start | bytes 393224 | tf_op jit(solution)/shard_map/while/body/eval_jaxpr/ppermute | solution.py:16
  368.8 14.1 %copy-start.2 = (f32[2,2,128,2,128]{4,3,2,1,0:T(2,128)S(1)}, f32[2,2,128,2,128]{4,3,2,1,0:T(2,128)}, u32[]{:S(2)}) copy-start(f32[2,2,128,2,128]{4,3,2,1,0:T(2,128)} %get-tuple-element.777) | copy-start | bytes 1572868 | tf_op jit(solution)/shard_map/while
  369.9 8.8 %collective-permute-start.2 = (bf16[2,2,128,1,128]{4,3,2,1,0:T(2,128)(2,1)}, bf16[2,2,128,1,128]{4,3,2,1,0:T(2,128)(2,1)S(1)}, u32[]{:S(2)}, u32[]{:S(2)}) collective-permute-start(bf16[2,2,128,1,128]{4,3,2,1,0:T(2,128)(2,1)} %get-tuple-element.775), channel_id=1, source_target_pairs={{4,0},{8,4},{12,8},{16,12},{20,16},{24,20},{28,24},{5,1},{9,5},{13... | collective-permute-start | bytes 393224 | tf_op jit(solution)/shard_map/while/body/eval_jaxpr/ppermute | solution.py:17
  371.2 10.9 %collective-permute-start.3 = (bf16[2,2,128,1,128]{4,3,2,1,0:T(2,128)(2,1)}, bf16[2,2,128,1,128]{4,3,2,1,0:T(2,128)(2,1)S(1)}, u32[]{:S(2)}, u32[]{:S(2)}) collective-permute-start(bf16[2,2,128,1,128]{4,3,2,1,0:T(2,128)(2,1)} %get-tuple-element.776), channel_id=1, source_target_pairs={{0,4},{4,8},{8,12},{12,16},{16,20},{20,24},{24,28},{1,5},{5,9},{9,... | collective-permute-start | bytes 393224 | tf_op jit(solution)/shard_map/while/body/eval_jaxpr/ppermute | solution.py:16
  390.6 14.9 %copy-start.2 = (f32[2,2,128,2,128]{4,3,2,1,0:T(2,128)S(1)}, f32[2,2,128,2,128]{4,3,2,1,0:T(2,128)}, u32[]{:S(2)}) copy-start(f32[2,2,128,2,128]{4,3,2,1,0:T(2,128)} %get-tuple-element.777) | copy-start | bytes 1572868 | tf_op jit(solution)/shard_map/while
  391.7 8.8 %collective-permute-start.2 = (bf16[2,2,128,1,128]{4,3,2,1,0:T(2,128)(2,1)}, bf16[2,2,128,1,128]{4,3,2,1,0:T(2,128)(2,1)S(1)}, u32[]{:S(2)}, u32[]{:S(2)}) collective-permute-start(bf16[2,2,128,1,128]{4,3,2,1,0:T(2,128)(2,1)} %get-tuple-element.775), channel_id=1, source_target_pairs={{4,0},{8,4},{12,8},{16,12},{20,16},{24,20},{28,24},{5,1},{9,5},{13... | collective-permute-start | bytes 393224 | tf_op jit(solution)/shard_map/while/body/eval_jaxpr/ppermute | solution.py:17
  393.0 11.6 %collective-permute-start.3 = (bf16[2,2,128,1,128]{4,3,2,1,0:T(2,128)(2,1)}, bf16[2,2,128,1,128]{4,3,2,1,0:T(2,128)(2,1)S(1)}, u32[]{:S(2)}, u32[]{:S(2)}) collective-permute-start(bf16[2,2,128,1,128]{4,3,2,1,0:T(2,128)(2,1)} %get-tuple-element.776), channel_id=1, source_target_pairs={{0,4},{4,8},{8,12},{12,16},{16,20},{20,24},{24,28},{1,5},{5,9},{9,... | collective-permute-start | bytes 393224 | tf_op jit(solution)/shard_map/while/body/eval_jaxpr/ppermute | solution.py:16
  412.2 22.9 %all-to-all-start.1 = ((bf16[2,256,256]{2,0,1:T(2,128)(2,1)}), bf16[2,256,256]{2,0,1:T(2,128)(2,1)S(1)}, u32[]{:S(2)}, u32[]{:S(2)}) async-start(bf16[2,256,256]{2,0,1:T(2,128)(2,1)} %reshape.142), calls=%async_computation.1 | async-start | bytes 524288 | tf_op jit(solution)/shard_map/all_to_all | solution.py:201
  435.1 22.4 %all-to-all-start = ((bf16[8,2,32768]{2,1,0:T(2,128)(2,1)}), bf16[8,2,32768]{2,1,0:T(2,128)(2,1)S(1)}, u32[]{:S(2)}, u32[]{:S(2)}) async-start(bf16[8,2,32768]{2,1,0:T(2,128)(2,1)} %reshape.143), calls=%async_computation | async-start | bytes 2097152 | tf_op jit(solution)/shard_map/all_to_all | solution.py:200
  (15 other events, 58.7 us)
Sparse Core Ops, SparseCore 0:
  11.9 73.2 all-reduce.3
  273.8 75.3 all-reduce.5
where the time goes:
time: 471 us; the launch traced here: 467 us
  waiting for transfers between devices  106 us (23%)
  local copies, waits for them, and re-layouts  94 us (20%)
  starting transfers between devices  89.1 us (19%)
  matrix products  75.1 us (16%)
  other arithmetic  71.6 us (15%)
  loops' own time  17.6 us (4%)
  between operations  14.3 us (3%)
    ppermute x12, starting transfers between devices, padded(): before = lax.ppermute(last, axis, up)  58.9 us
    ppermute x12, waiting for transfers between devices, padded(): after = lax.ppermute(leading, axis, down)  53.4 us
    ppermute x12, waiting for transfers between devices, padded(): before = lax.ppermute(last, axis, up)  37.4 us
    dot_general x8, matrix products, output_step(): jnp.einsum('ahgit,athd->aihgd', attn_probs.astype(jnp.bfloat16), key_valu...  28.3 us
    squeeze x24, local copies, waits for them, and re-layouts, per_device(): lax.scan(stats_step, (jnp.full(stats_shape, -jnp.inf, jnp.float32), jnp.z...  23.4 us
    dot_general x16, matrix products, scores_of(): jnp.einsum('aihgd,athd->ahgit', query_side, key_side, preferred_element_t...  19.4 us
    dynamic_slice x12, local copies, waits for them, and re-layouts, per_device(): returned = lax.scan(climb_back, key_zero, key_parts[2:], reverse=True)[0]  18.9 us
    ppermute x12, starting transfers between devices, padded(): after = lax.ppermute(leading, axis, down)  15.4 us
  transfers between devices with their start and end apart: 28, of which 25 were waited for; matrix products, arithmetic and copies ran while one was open for 19% of the time, Pallas kernels for 0%

commit v1 on v0

v1 whole, which is shorter than its diff:
```python
import functools
import math

import jax
import jax.numpy as jnp
from jax import lax
from jax.experimental import pallas as pl
from jax.experimental.pallas import tpu as pltpu
from jax.sharding import PartitionSpec as P

NN = (((1,), (0,)), ((), ()))
NT = (((1,), (1,)), ((), ()))


def dot(a, b, dims):
    return lax.dot_general(a, b, dims, preferred_element_type=jnp.float32)


def attention_kernel(
    shape,
    blocks_ref,
    places_ref,
    listed_ref,
    q_ref,
    do_ref,
    k_ref,
    v_ref,
    dq_ref,
    dkv_ref,
    kcat,
    vcat,
    kcat_t,
    bias,
    dk_acc,
    dv_acc,
    total,
):
    block_len, head_dim, group_size, slots = shape
    scale = 1.0 / math.sqrt(head_dim)
    a = pl.program_id(1)
    wide = 2 * block_len

    @pl.when(a == 0)
    def _():
        total[...] = jnp.zeros_like(total)

    for j in range(slots):
        rows = pl.ds(pl.multiple_of(blocks_ref[a, j] * block_len, block_len), block_len)
        here = pl.ds(j * block_len, block_len)
        kcat[here, :] = k_ref[rows, :]
        vcat[here, :] = v_ref[rows, :]
        kcat_t[:, here] = k_ref[rows, :].T
        off = jnp.where(listed_ref[a, j] > 0, 0.0, -jnp.inf)
        if j == 0:
            key_at = lax.broadcasted_iota(jnp.int32, (block_len, wide), 0)
            query_at = lax.broadcasted_iota(jnp.int32, (block_len, wide), 1) % block_len
            bias[here, :] = jnp.where(key_at <= query_at, 0.0, -jnp.inf)
        else:
            bias[here, :] = jnp.full((block_len, wide), off, jnp.float32)

    keys = slots * block_len

    def pair(i, carry):
        def two(ref):
            return [
                ref[:, pl.ds(pl.multiple_of((2 * i + e) * head_dim, head_dim), head_dim)]
                for e in range(2)
            ]

        q2 = jnp.concatenate(two(q_ref), axis=0)
        do2 = jnp.concatenate(two(do_ref), axis=0)
        scores = dot(kcat[...], q2, NT) * scale + bias[...]
        grad_probs = dot(vcat[...], do2, NT)
        row_max = jnp.max(scores, axis=0, keepdims=True)
        weights = jnp.exp(scores - row_max)
        probs = weights * (1.0 / jnp.sum(weights, axis=0, keepdims=True))
        low = probs.astype(jnp.bfloat16)
        delta = jnp.sum(low.astype(jnp.float32) * grad_probs, axis=0, keepdims=True)
        grad_scores = (probs * (grad_probs - delta)).astype(jnp.bfloat16)
        dq = (dot(kcat_t[...], grad_scores, NN) * scale).astype(jnp.bfloat16)
        for e in range(2):
            rows = pl.ds(pl.multiple_of((2 * i + e) * head_dim, head_dim), head_dim)
            dq_ref[rows, :] = dq[:, e * block_len : (e + 1) * block_len]
        dk = dot(grad_scores, q2, NN)
        dv = dot(low, do2, NN)

        @pl.when(i == 0)
        def _():
            dk_acc[...] = dk
            dv_acc[...] = dv

        @pl.when(i > 0)
        def _():
            dk_acc[...] += dk
            dv_acc[...] += dv

        return carry

    lax.fori_loop(0, group_size // 2, pair, 0)

    for j in range(slots):
        here = pl.ds(j * block_len, block_len)
        b = places_ref[a, j]
        total[0, b] += (dk_acc[here, :] * scale).T
        total[1, b] += dv_acc[here, :].T

    @pl.when(a == 1)
    def _():
        for b in range(total.shape[1]):
            here = pl.ds(b * block_len, block_len)
            dkv_ref[0, :, here] = total[0, b].astype(jnp.bfloat16)
            dkv_ref[1, :, here] = total[1, b].astype(jnp.bfloat16)


def per_device(queries, key_vectors, values, grad_out, key_blocks):
    n = lax.axis_size("seq")
    me = lax.axis_index("seq")
    tokens, q_heads, head_dim = queries.shape
    block_len = tokens // 2
    kv_heads = key_vectors.shape[1]
    group_size = q_heads // kv_heads
    slots = key_blocks.shape[1]
    window = slots - 2
    blocks = 2 * n

    kv = jnp.concatenate(
        [key_vectors.reshape(tokens, -1), values.reshape(tokens, -1)], axis=1
    )
    kv_all = lax.all_gather(kv, "seq", axis=0, tiled=True)

    positions = jnp.stack([me, blocks - 1 - me])
    back = jnp.concatenate(
        [jnp.zeros((1,), jnp.int32), jnp.arange(1, window + 1, dtype=jnp.int32)]
    )
    near = positions[:, None] - back[None, :]
    near_hit = jnp.any(key_blocks[:, None, :] == near[:, :, None], axis=2) & (near >= 0)
    sink_hit = jnp.any(key_blocks == 0, axis=1) & (positions > window)
    listed = jnp.concatenate([near_hit, sink_hit[:, None]], axis=1).astype(jnp.int32)
    wanted = jnp.concatenate(
        [jnp.maximum(near, 0), jnp.zeros((2, 1), jnp.int32)], axis=1
    )
    stored = jnp.where(wanted < n, 2 * wanted, 2 * (blocks - 1 - wanted) + 1).astype(jnp.int32)

    dense = blocks <= 2 * slots
    count = blocks if dense else 2 * slots
    places = stored if dense else jnp.arange(count, dtype=jnp.int32).reshape(2, slots)
    keys = slots * block_len
    width = group_size * head_dim
    shape = (block_len, head_dim, group_size, slots)
    f32, bf16 = jnp.float32, jnp.bfloat16
    dq, dkv = pl.pallas_call(
        functools.partial(attention_kernel, shape),
        grid_spec=pltpu.PrefetchScalarGridSpec(
            num_scalar_prefetch=3,
            grid=(kv_heads, 2),
            in_specs=[
                pl.BlockSpec((block_len, width), lambda g, a, *_: (a, g)),
                pl.BlockSpec((block_len, width), lambda g, a, *_: (a, g)),
                pl.BlockSpec((n * tokens, head_dim), lambda g, a, *_: (0, g)),
                pl.BlockSpec((n * tokens, head_dim), lambda g, a, *_: (0, kv_heads + g)),
            ],
            out_specs=[
                pl.BlockSpec((width, block_len), lambda g, a, *_: (g, a)),
                pl.BlockSpec((2, head_dim, count * block_len), lambda g, a, *_: (0, g, 0)),
            ],
            scratch_shapes=[
                pltpu.VMEM((keys, head_dim), bf16),
                pltpu.VMEM((keys, head_dim), bf16),
                pltpu.VMEM((head_dim, keys), bf16),
                pltpu.VMEM((keys, 2 * block_len), f32),
                pltpu.VMEM((keys, head_dim), f32),
                pltpu.VMEM((keys, head_dim), f32),
                pltpu.VMEM((2, count, head_dim, block_len), f32),
            ],
        ),
        out_shape=[
            jax.ShapeDtypeStruct((q_heads * head_dim, tokens), bf16),
            jax.ShapeDtypeStruct((2, kv_heads * head_dim, count * block_len), bf16),
        ],
        name="attention_backward",
    )(
        stored,
        places,
        listed,
        queries.reshape(tokens, -1),
        grad_out.reshape(tokens, -1),
        kv_all,
        kv_all,
    )
    dq_rows = lax.all_to_all(dq, "seq", split_axis=0, concat_axis=1, tiled=True)
    rows = kv_heads * head_dim // n
    parts = lax.all_to_all(
        dkv.reshape(2, n, rows, count * block_len), "seq", split_axis=1, concat_axis=1, tiled=True
    )
    if dense:
        dkv_rows = jnp.sum(parts.astype(f32), axis=1).astype(bf16)
    else:
        dkv_rows = placed(parts.reshape(2, n, rows, 2, slots, block_len)).astype(bf16)
    return (dq_rows, dkv_rows[0], dkv_rows[1])


def placed(parts):
    kinds, n, rows, _, slots, block_len = parts.shape
    by_position = jnp.concatenate([parts[:, :, :, 0], parts[:, ::-1, :, 1]], axis=1)
    by_position = by_position.astype(jnp.float32)
    total = by_position[:, :, :, 0]
    for back in range(1, slots - 1):
        total = total.at[:, : 2 * n - back].add(by_position[:, back:, :, back])
    total = total.at[:, 0].add(jnp.sum(by_position[:, :, :, slots - 1], axis=1))
    stored = jnp.stack([total[:, :n], total[:, n:][:, ::-1]], axis=2)
    stored = stored.reshape(kinds, 2 * n, rows, block_len)
    return jnp.transpose(stored, (0, 2, 1, 3)).reshape(kinds, rows, 2 * n * block_len)


def solution(mesh):
    return jax.shard_map(
        per_device,
        mesh=mesh,
        in_specs=(
            P("seq", "head", None),
            P("seq", "head", None),
            P("seq", "head", None),
            P("seq", "head", None),
            P("seq", None),
        ),
        out_specs=(P(("head", "seq"), None), P(("head", "seq"), None), P(("head", "seq"), None)),
        check_vma=False,
    )
```

time: 471 us -> 181 us (0.38)
  local copies, waits for them, and re-layouts: 94 us -> 7.77 us
  starting transfers between devices: 89.1 us -> 7.33 us
  matrix products: 75.1 us -> 0 us
  other arithmetic: 71.6 us -> 4.31 us
  Pallas kernels: 0 us -> 30.2 us
  loops' own time: 17.6 us -> 0 us
  waiting for transfers between devices: 106 us -> 117 us
    ppermute x24 -> x0, waiting for transfers between devices: 90.8 us -> none  [the longest x12 53.4 us: padded(): after = lax.ppermute(leading, axis, down)]
    dot_general x56 -> x0, matrix products: 75.1 us -> none  [the longest x8 28.3 us: output_step(): jnp.einsum('ahgit,athd->aihgd', attn_probs.astype(jnp.bfloat16), key_valu...]
    ppermute x24 -> x0, starting transfers between devices: 74.3 us -> none  [the longest x12 58.9 us: padded(): before = lax.ppermute(last, axis, up)]
    all_to_all x2, waiting for transfers between devices: 15 us -> 70.6 us  [the longest x1 47.1 us: per_device(): lax.all_to_all(dkv.reshape(2, n, rows, count * block_len), 'seq', split_a...]
    all_gather x0 -> x1, waiting for transfers between devices: none -> 46.3 us  [per_device(): kv_all = lax.all_gather(kv, 'seq', axis=0, tiled=True)]
    dynamic_slice x36 -> x0, local copies, waits for them, and re-layouts: 33 us -> none  [the longest x12 18.9 us: per_device(): returned = lax.scan(climb_back, key_zero, key_parts[2:], reverse=True)[0]]
    pallas_call x0 -> x1, Pallas kernels: none -> 30.2 us  [per_device(): pl.pallas_call(functools.partial(attention_kernel, shape), grid_spec=pltp...]
    squeeze x24 -> x1, local copies, waits for them, and re-layouts: 23.4 us -> 0.72 us  [per_device(): return (dq_rows, dkv_rows[0], dkv_rows[1])]
  transfers between devices with their start and end apart: 28 -> 3, of which waited for: 25 -> 3; matrix products, arithmetic and copies ran while one was open for 19% -> 5% of each run, Pallas kernels for 0% -> 0%
where the time goes in v1:
time: 181 us
  waiting for transfers between devices  117 us (65%)
  Pallas kernels  30.2 us (17%)
  between operations  14.1 us (8%)
  local copies, waits for them, and re-layouts  7.77 us (4%)
  starting transfers between devices  7.33 us (4%)
  other arithmetic  4.31 us (2%)
    all_to_all x1, waiting for transfers between devices, per_device(): lax.all_to_all(dkv.reshape(2, n, rows, count * block_len), 'seq', split_a...  47.1 us
    all_gather x1, waiting for transfers between devices, per_device(): kv_all = lax.all_gather(kv, 'seq', axis=0, tiled=True)  46.3 us
    pallas_call x1, Pallas kernels, per_device(): pl.pallas_call(functools.partial(attention_kernel, shape), grid_spec=pltp...  30.2 us
    all_to_all x1, waiting for transfers between devices, per_device(): dq_rows = lax.all_to_all(dq, 'seq', split_axis=0, concat_axis=1, tiled=True)  23.5 us
    all_to_all x1, starting transfers between devices, per_device(): dq_rows = lax.all_to_all(dq, 'seq', split_axis=0, concat_axis=1, tiled=True)  3.69 us
  transfers between devices with their start and end apart: 3, of which 3 were waited for; matrix products, arithmetic and copies ran while one was open for 5% of the time, Pallas kernels for 0%

profile of v1, /device:TPU:0, one launch (start us, length us, event | category | flops | bytes accessed | tf_op | source)
XLA Modules:
  0.0 180.6 jit_solution(10384565207261479372)
XLA Ops:
  7.2 0.0 all-gather.2.cloned.1.call-start
  7.2 1.0 copy_bitcast_fusion.2
  8.2 0.7 pad_maximum_fusion
  8.9 0.0 all-gather.2.cloned.1.call-update
  9.0 0.8 compare_reduce_fusion.1
  9.8 0.1 copy.13
  9.9 0.1 pad_add_fusion
  10.0 0.1 pad_add_fusion.1
  10.0 0.1 broadcast_subtract_fusion
  10.1 0.6 compare_select_fusion.blocks_ref.places_ref
  10.7 0.9 compare_reduce_fusion
  11.6 0.1 compare_and_fusion.1
  11.7 0.6 add_convert_fusion.listed_ref
  12.3 3.4 %copy_bitcast_fusion = (bf16[256,2048]{1,0:T(8,128)(2,1)}, bf16[256,2048]{1,0:T(8,128)(2,1)}) fusion(bf16[32,8,16,128]{3,2,1,0:T(8,128)(2,1)} %bitcast.30, bf16[32,8,16,128]{3,2,1,0:T(8,128)(2,1)} %bitcast.31), kind=kLoop, calls=%fused_computation | loop fusion | bytes 4194304 | tf_op jit(solution)/shard_map/reshape | solution.py:186
  15.7 46.3 %all-gather.2.cloned.1.call-done.k_ref.v_ref = bf16[2048,512]{1,0:T(8,128)(2,1)} async-done(((bf16[256,512]{1,0:T(8,128)(2,1)}), bf16[2048,512]{1,0:T(8,128)(2,1)}) %all-gather.2.cloned.1.call-update) | async-done | bytes 2097168 | tf_op jit(solution)/shard_map/all_gather | solution.py:129
  61.9 30.2 %attention_backward.1 = (bf16[2048,256]{1,0:T(8,128)(2,1)}, bf16[2,256,2048]{2,1,0:T(8,128)(2,1)}) custom-call(s32[2,8]{1,0:T(2,128)} %compare_select_fusion.blocks_ref.places_ref, s32[2,8]{1,0:T(2,128)} %compare_select_fusion.blocks_ref.places_ref, s32[2,8]{1,0:T(2,128)} %add_convert_fusion.listed_ref, bf16[256,2048]{1,0:T(8,128)(2,1)} %get-tuple-element.14.q_ref, ...), custom_call_target="tpu_custom_call" | custom-call | tf_op jit(solution)/shard_map/attention_backward/pallas_call | solution.py:151
  92.2 0.0 copy-start
  92.2 3.7 %all-to-all-start = ((bf16[8,256,256]{2,1,0:T(8,128)(2,1)}), bf16[8,256,256]{2,1,0:T(8,128)(2,1)S(1)}, u32[]{:S(2)}, u32[]{:S(2)}) async-start(bf16[8,256,256]{2,1,0:T(8,128)(2,1)} %bitcast.29), calls=%async_computation | async-start | bytes 2097152 | tf_op jit(solution)/shard_map/all_to_all | solution.py:190
  95.9 0.0 copy-done
  95.9 1.5 copy.15
  97.3 23.5 %all-to-all-done = bf16[8,256,256]{2,1,0:T(8,128)(2,1)S(1)} async-done(((bf16[8,256,256]{2,1,0:T(8,128)(2,1)}), bf16[8,256,256]{2,1,0:T(8,128)(2,1)S(1)}, u32[]{:S(2)}, u32[]{:S(2)}) %all-to-all-start) | async-done | bytes 1048608 | tf_op jit(solution)/shard_map/all_to_all | solution.py:190
  120.8 3.6 %all-to-all-start.1 = ((bf16[2,8,32,2048]{3,2,0,1:T(8,128)(2,1)}), bf16[2,8,32,2048]{3,2,0,1:T(8,128)(2,1)S(1)}, u32[]{:S(2)}, u32[]{:S(2)}) async-start(bf16[2,8,32,2048]{3,2,0,1:T(8,128)(2,1)} %copy.15), calls=%async_computation.1 | async-start | bytes 4194304 | tf_op jit(solution)/shard_map/all_to_all | solution.py:192
  124.5 1.1 copy.16
  125.6 47.1 %all-to-all-done.1 = bf16[2,8,32,2048]{3,2,0,1:T(8,128)(2,1)S(1)} async-done(((bf16[2,8,32,2048]{3,2,0,1:T(8,128)(2,1)}), bf16[2,8,32,2048]{3,2,0,1:T(8,128)(2,1)S(1)}, u32[]{:S(2)}, u32[]{:S(2)}) %all-to-all-start.1) | async-done | bytes 2097184 | tf_op jit(solution)/shard_map/all_to_all | solution.py:192
  172.6 0.4 reduce_sum.12
  173.0 0.7 slice_bitcast_fusion
  (2 shorter events, 0.0 us)
Async XLA Ops:
  7.2 54.8 %all-gather.2.cloned.1.call-start = ((), (), s32[]{:S(2)}) async-start(), calls=%async_computation.2 | async-start | bytes 2359296 | tf_op jit(solution)/shard_map/all_gather | solution.py:129
  92.2 3.7 %copy-start = (bf16[2,256,2048]{2,1,0:T(8,128)(2,1)S(1)}, bf16[2,256,2048]{2,1,0:T(8,128)(2,1)}, u32[]{:S(2)}) copy-start(bf16[2,256,2048]{2,1,0:T(8,128)(2,1)} %get-tuple-element.6) | copy-start | bytes 6291460
  92.2 28.7 %all-to-all-start = ((bf16[8,256,256]{2,1,0:T(8,128)(2,1)}), bf16[8,256,256]{2,1,0:T(8,128)(2,1)S(1)}, u32[]{:S(2)}, u32[]{:S(2)}) async-start(bf16[8,256,256]{2,1,0:T(8,128)(2,1)} %bitcast.29), calls=%async_computation | async-start | bytes 2097152 | tf_op jit(solution)/shard_map/all_to_all | solution.py:190
  120.8 51.8 %all-to-all-start.1 = ((bf16[2,8,32,2048]{3,2,0,1:T(8,128)(2,1)}), bf16[2,8,32,2048]{3,2,0,1:T(8,128)(2,1)S(1)}, u32[]{:S(2)}, u32[]{:S(2)}) async-start(bf16[2,8,32,2048]{3,2,0,1:T(8,128)(2,1)} %copy.15), calls=%async_computation.1 | async-start | bytes 4194304 | tf_op jit(solution)/shard_map/all_to_all | solution.py:192
Sparse Core Ops, SparseCore 0:
  10.1 51.7 all-gather.1

commit v2 on v1

--- a/solution.py
+++ b/solution.py
@@ -112,6 +112,381 @@
             dkv_ref[1, :, here] = total[1, b].astype(jnp.bfloat16)
 
 
+def fused_kernel(
+    sizes,
+    listed_ref,
+    q_ref,
+    do_ref,
+    kv_ref,
+    dq_out,
+    dk_out,
+    dv_out,
+    kv_at,
+    kcat,
+    vcat,
+    kcat_t,
+    bias,
+    dk_acc,
+    dv_acc,
+    total,
+    dq_stage,
+    stage,
+    arrived,
+    row_sum,
+    kv_send,
+    kv_recv,
+    dq_send,
+    dq_recv,
+    part_send,
+    part_recv,
+):
+    n, block_len, head_dim, kv_heads, group_size, slots = sizes
+    window = slots - 2
+    blocks = 2 * n
+    pairs = group_size // 2
+    per_kv = n // kv_heads
+    rows = kv_heads * head_dim // n
+    wide = 2 * block_len
+    scale = 1.0 / math.sqrt(head_dim)
+    bf16, f32 = jnp.bfloat16, jnp.float32
+    me = lax.axis_index("seq")
+    mine = (me, blocks - 1 - me)
+
+    def used(device, position):
+        top = blocks - 1 - device
+        return (
+            ((position <= device) & (position >= device - window))
+            | ((position <= top) & (position >= top - window))
+            | (position == 0)
+        )
+
+    def remote(src, dst, send, recv, device):
+        return pltpu.make_async_remote_copy(
+            src_ref=src,
+            dst_ref=dst,
+            send_sem=send,
+            recv_sem=recv,
+            device_id={"seq": device},
+            device_id_type=pl.DeviceIdType.MESH,
+        )
+
+    barrier = pltpu.get_barrier_semaphore()
+    for step in range(1, n):
+        pl.semaphore_signal(
+            barrier,
+            inc=1,
+            device_id={"seq": lax.rem(me + step, n)},
+            device_id_type=pl.DeviceIdType.MESH,
+        )
+    pl.semaphore_wait(barrier, n - 1)
+
+    def kv_copy(half, device):
+        return remote(
+            kv_ref.at[pl.ds(half * block_len, block_len), :],
+            kv_at.at[mine[half]],
+            kv_send.at[half, device],
+            kv_recv.at[mine[half]],
+            device,
+        )
+
+    far_first = sorted(range(1, n), key=lambda step: -min(step, n - step))
+    for half in range(2):
+        for step in far_first:
+            device = lax.rem(me + step, n)
+
+            @pl.when(used(device, mine[half]))
+            def _():
+                kv_copy(half, device).start()
+
+    for half in range(2):
+        kv_at[mine[half]] = kv_ref[pl.ds(half * block_len, block_len), :]
+
+    def kv_wait(position):
+        remote(
+            kv_ref.at[pl.ds(0, block_len), :],
+            kv_at.at[position],
+            kv_send.at[0, me],
+            kv_recv.at[position],
+            me,
+        ).wait_recv()
+
+    def dq_copy(g, a, i):
+        device = g * per_kv + i
+        return device, remote(
+            dq_stage.at[a, pl.ds(pl.multiple_of(device * wide, wide), wide), :],
+            dq_out.at[:, pl.ds(pl.multiple_of(me * wide + a * block_len, block_len), block_len)],
+            dq_send.at[a, device],
+            dq_recv.at[a, me],
+            device,
+        )
+
+    def dq_start(g, a, i):
+        device, copy = dq_copy(g, a, i)
+
+        @pl.when(device != me)
+        def _():
+            copy.start()
+
+    def part_copy(g, e, b):
+        device = g * per_kv + e
+        return device, remote(
+            stage.at[g, b, :, pl.ds(pl.multiple_of(e * rows, rows), rows), :],
+            arrived.at[me, b],
+            part_send.at[device, b],
+            part_recv.at[me, b],
+            device,
+        )
+
+    def wanted(a, j):
+        top = jnp.where(a == 0, mine[0], mine[1])
+        if j == slots - 1:
+            return jnp.int32(0) * top
+        return jnp.maximum(top - j, 0)
+
+    def attend(g, a):
+        columns = pl.ds(pl.multiple_of(g * head_dim, head_dim), head_dim)
+        v_columns = pl.ds(pl.multiple_of((kv_heads + g) * head_dim, head_dim), head_dim)
+        for j in range(slots):
+            here = pl.ds(j * block_len, block_len)
+            position = wanted(a, j)
+            k_block = kv_at[position, :, columns]
+            kcat[here, :] = k_block
+            vcat[here, :] = kv_at[position, :, v_columns]
+            kcat_t[:, here] = k_block.T
+            if j == 0:
+                key_at = lax.broadcasted_iota(jnp.int32, (block_len, wide), 0)
+                query_at = lax.broadcasted_iota(jnp.int32, (block_len, wide), 1) % block_len
+                bias[here, :] = jnp.where(key_at <= query_at, 0.0, -jnp.inf)
+            else:
+                off = jnp.where(listed_ref[a, j] > 0, 0.0, -jnp.inf)
+                bias[here, :] = jnp.full((block_len, wide), off, f32)
+        dk_acc[...] = jnp.zeros_like(dk_acc)
+        dv_acc[...] = jnp.zeros_like(dv_acc)
+        query_rows = pl.ds(pl.multiple_of(a * block_len, block_len), block_len)
+
+        def pair(i, carry):
+            @pl.when(i > 0)
+            def _():
+                dq_start(g, a, i - 1)
+
+            first = g * group_size + 2 * i
+
+            def two(ref):
+                return jnp.concatenate(
+                    [
+                        ref[
+                            query_rows,
+                            pl.ds(pl.multiple_of((first + e) * head_dim, head_dim), head_dim),
+                        ]
+                        for e in range(2)
+                    ],
+                    axis=0,
+                )
+
+            q2 = two(q_ref)
+            do2 = two(do_ref)
+            scores = dot(kcat[...], q2, NT) * scale + bias[...]
+            grad_probs = dot(vcat[...], do2, NT)
+            row_max = jnp.max(scores, axis=0, keepdims=True)
+            weights = jnp.exp(scores - row_max)
+            probs = weights * (1.0 / jnp.sum(weights, axis=0, keepdims=True))
+            low = probs.astype(bf16)
+            delta = jnp.sum(low.astype(f32) * grad_probs, axis=0, keepdims=True)
+            grad_scores = (probs * (grad_probs - delta)).astype(bf16)
+            dq = (dot(kcat_t[...], grad_scores, NN) * scale).astype(bf16)
+            for e in range(2):
+                at = pl.ds(pl.multiple_of((first + e) * head_dim, head_dim), head_dim)
+                dq_stage[a, at, :] = dq[:, e * block_len : (e + 1) * block_len]
+            dk_acc[...] += dot(grad_scores, q2, NN)
+            dv_acc[...] += dot(low, do2, NN)
+            return carry
+
+        lax.fori_loop(0, pairs, pair, 0)
+        for j in range(slots):
+            here = pl.ds(j * block_len, block_len)
+            position = wanted(a, j)
+            total[position, 0] += (dk_acc[here, :] * scale).T
+            total[position, 1] += dv_acc[here, :].T
+        dq_start(g, a, pairs - 1)
+
+    def step_of(step, carry):
+        phase, a = step // 2, lax.rem(step, 2)
+        far = 1 - me // (n // 2)
+        g = jnp.where(phase == 0, far, 1 - far)
+
+        def arrivals(position, c):
+            low_part = (
+                (position <= me) & (position >= me - window) | (position == 0)
+            )
+            due = jnp.where(a == 0, low_part, used(me, position) & jnp.logical_not(low_part))
+            other = (position != mine[0]) & (position != mine[1])
+
+            @pl.when(due & other & (phase == 0))
+            def _():
+                kv_wait(position)
+
+            return c
+
+        lax.fori_loop(0, blocks, arrivals, 0)
+
+        @pl.when(a == 0)
+        def _():
+            total[...] = jnp.zeros_like(total)
+
+        attend(g, a)
+
+        @pl.when(a == 1)
+        def _():
+            def finish(b, c):
+                @pl.when(used(me, b))
+                def _():
+                    stage[g, b] = total[b].astype(bf16)
+
+                return c
+
+            lax.fori_loop(0, blocks, finish, 0)
+
+            def send(b, c):
+                for e in range(per_kv):
+                    device, copy = part_copy(g, e, b)
+
+                    @pl.when(used(me, b) & (device != me))
+                    def _():
+                        copy.start()
+
+                return c
+
+            lax.fori_loop(0, blocks, send, 0)
+
+        return carry
+
+    lax.fori_loop(0, 2 * kv_heads, step_of, 0)
+
+    own_rows = pl.ds(pl.multiple_of(me * wide, wide), wide)
+    for a in range(2):
+        at = pl.ds(pl.multiple_of(me * wide + a * block_len, block_len), block_len)
+        dq_out[:, at] = dq_stage[a, own_rows, :]
+
+    own_g = me // per_kv
+    part_rows = pl.ds(pl.multiple_of(lax.rem(me, per_kv) * rows, rows), rows)
+
+    def own(b, c):
+        row_sum[b] = jnp.zeros(row_sum.shape[1:], f32)
+
+        @pl.when(used(me, b))
+        def _():
+            row_sum[b] = stage[own_g, b, :, part_rows, :].astype(f32)
+
+        return c
+
+    lax.fori_loop(0, blocks, own, 0)
+
+    def gather(step, carry):
+        source = lax.rem(me + step, n)
+
+        def one(b, c):
+            @pl.when(used(source, b))
+            def _():
+                remote(
+                    stage.at[0, b, :, pl.ds(0, rows), :],
+                    arrived.at[source, b],
+                    part_send.at[source, b],
+                    part_recv.at[source, b],
+                    source,
+                ).wait_recv()
+                row_sum[b] += arrived[source, b].astype(f32)
+
+            return c
+
+        lax.fori_loop(0, blocks, one, 0)
+        return carry
+
+    lax.fori_loop(1, n, gather, 0)
+    for b in range(blocks):
+        at = 2 * b if b < n else 2 * (blocks - 1 - b) + 1
+        here = pl.ds(at * block_len, block_len)
+        dk_out[:, here] = row_sum[b, 0].astype(bf16)
+        dv_out[:, here] = row_sum[b, 1].astype(bf16)
+
+    def finish_dq(step, carry):
+        other = lax.rem(me + step, n)
+        for a in range(2):
+            remote(
+                dq_stage.at[a, pl.ds(0, wide), :],
+                dq_out.at[:, pl.ds(pl.multiple_of(other * wide + a * block_len, block_len), block_len)],
+                dq_send.at[a, other],
+                dq_recv.at[a, other],
+                other,
+            ).wait_recv()
+            dq_copy(0, a, other)[1].wait_send()
+        for half in range(2):
+
+            @pl.when(used(other, mine[half]))
+            def _():
+                kv_copy(half, other).wait_send()
+
+        def sent(b, c):
+            @pl.when(used(me, b))
+            def _():
+                remote(
+                    stage.at[0, b, :, pl.ds(0, rows), :],
+                    arrived.at[me, b],
+                    part_send.at[other, b],
+                    part_recv.at[me, b],
+                    other,
+                ).wait_send()
+
+            return c
+
+        lax.fori_loop(0, blocks, sent, 0)
+        return carry
+
+    lax.fori_loop(1, n, finish_dq, 0)
+
+
+def fused(queries, grad_out, kv, listed, sizes):
+    n, block_len, head_dim, kv_heads, group_size, slots = sizes
+    blocks = 2 * n
+    keys = slots * block_len
+    tokens = 2 * block_len
+    rows = kv_heads * head_dim // n
+    f32, bf16 = jnp.float32, jnp.bfloat16
+    dma = pltpu.SemaphoreType.DMA
+    vmem = pl.BlockSpec(memory_space=pltpu.VMEM)
+    return pl.pallas_call(
+        functools.partial(fused_kernel, sizes),
+        in_specs=[pl.BlockSpec(memory_space=pltpu.SMEM), vmem, vmem, vmem],
+        out_specs=[vmem] * 3,
+        out_shape=[
+            jax.ShapeDtypeStruct((kv_heads * group_size * head_dim // n, n * tokens), bf16),
+            jax.ShapeDtypeStruct((rows, n * tokens), bf16),
+            jax.ShapeDtypeStruct((rows, n * tokens), bf16),
+        ],
+        scratch_shapes=[
+            pltpu.VMEM((blocks, block_len, 2 * kv_heads * head_dim), bf16),
+            pltpu.VMEM((keys, head_dim), bf16),
+            pltpu.VMEM((keys, head_dim), bf16),
+            pltpu.VMEM((head_dim, keys), bf16),
+            pltpu.VMEM((keys, 2 * block_len), f32),
+            pltpu.VMEM((keys, head_dim), f32),
+            pltpu.VMEM((keys, head_dim), f32),
+            pltpu.VMEM((blocks, 2, head_dim, block_len), f32),
+            pltpu.VMEM((2, kv_heads * group_size * head_dim, block_len), bf16),
+            pltpu.VMEM((kv_heads, blocks, 2, head_dim, block_len), bf16),
+            pltpu.VMEM((n, blocks, 2, rows, block_len), bf16),
+            pltpu.VMEM((blocks, 2, rows, block_len), f32),
+            dma((2, n)),
+            dma((blocks,)),
+            dma((2, n)),
+            dma((2, n)),
+            dma((n, blocks)),
+            dma((n, blocks)),
+        ],
+        compiler_params=pltpu.CompilerParams(collective_id=0, has_side_effects=True),
+        name="attention_backward_exchange",
+    )(listed, queries, grad_out, kv)
+
+
 def per_device(queries, key_vectors, values, grad_out, key_blocks):
     n = lax.axis_size("seq")
     me = lax.axis_index("seq")
@@ -126,8 +501,6 @@
     kv = jnp.concatenate(
         [key_vectors.reshape(tokens, -1), values.reshape(tokens, -1)], axis=1
     )
-    kv_all = lax.all_gather(kv, "seq", axis=0, tiled=True)
-
     positions = jnp.stack([me, blocks - 1 - me])
     back = jnp.concatenate(
         [jnp.zeros((1,), jnp.int32), jnp.arange(1, window + 1, dtype=jnp.int32)]
@@ -144,6 +517,14 @@
     dense = blocks <= 2 * slots
     count = blocks if dense else 2 * slots
     places = stored if dense else jnp.arange(count, dtype=jnp.int32).reshape(2, slots)
+    if dense and kv_heads == 2 and q_heads == 2 * n and n % 2 == 0:
+        sizes = (n, block_len, head_dim, kv_heads, group_size, slots)
+        return tuple(
+            fused(
+                queries.reshape(tokens, -1), grad_out.reshape(tokens, -1), kv, listed, sizes
+            )
+        )
+    kv_all = lax.all_gather(kv, "seq", axis=0, tiled=True)
     keys = slots * block_len
     width = group_size * head_dim
     shape = (block_len, head_dim, group_size, slots)

time: 181 us -> 112 us (0.62)
  the two profiles are of different devices: /device:TPU:0 before, /device:TPU:22 now
where the time goes in v2:
time: 112 us; the launch traced here: 110 us
  Pallas kernels  97.9 us (87%)
  local copies, waits for them, and re-layouts  8.12 us (7%)
  other arithmetic  3.48 us (3%)
    pallas_call x1, Pallas kernels, fused(): pl.pallas_call(functools.partial(fused_kernel, sizes), in_specs=[pl.Block...  97.9 us
    unnamed x9, local copies, waits for them, and re-layouts  3.95 us
    reshape x1, local copies, waits for them, and re-layouts, per_device(): grad_out.reshape(tokens, -1)  3.06 us

profile of v2, /device:TPU:22, one launch (start us, length us, event | category | flops | bytes accessed | tf_op | source)
XLA Modules:
  0.0 110.2 jit_solution(17934771508014810759)
XLA Ops:
  0.6 0.0 copy-start
  0.6 0.1 pad_add_fusion
  0.7 0.9 compare_reduce_fusion.1
  1.6 0.1 copy.9
  1.7 0.1 pad_add_fusion.1
  1.8 0.1 broadcast_subtract_fusion
  1.9 0.9 compare_reduce_fusion
  2.8 0.1 compare_and_fusion.1
  2.8 0.6 add_convert_fusion.listed_ref
  3.5 1.0 copy_bitcast_fusion.2
  4.5 0.8 pad_maximum_fusion.kv_ref
  5.2 0.0 copy-done
  5.3 3.1 %copy_bitcast_fusion = (bf16[256,2048]{1,0:T(8,128)(2,1)}, bf16[256,2048]{1,0:T(8,128)(2,1)}) fusion(bf16[32,8,16,128]{3,2,1,0:T(8,128)(2,1)S(1)} %bitcast.17, bf16[32,8,16,128]{3,2,1,0:T(8,128)(2,1)} %bitcast.18), kind=kLoop, calls=%fused_computation | loop fusion | bytes 4194304 | tf_op jit(solution)/shard_map/reshape | solution.py:524
  8.3 97.9 %attention_backward_exchange.1 = (bf16[256,2048]{1,0:T(8,128)(2,1)}, bf16[32,2048]{1,0:T(8,128)(2,1)}, bf16[32,2048]{1,0:T(8,128)(2,1)}) custom-call(s32[2,8]{1,0:T(2,128)} %add_convert_fusion.listed_ref, bf16[256,2048]{1,0:T(8,128)(2,1)} %get-tuple-element.6.q_ref, bf16[256,2048]{1,0:T(8,128)(2,1)} %get-tuple-element.5.do_ref, ...), custom_call_target="tpu_custom_call" | custom-call | tf_op jit(solution)/shard_map/attention_backward_exchange/pallas_call | solution.py:456
  106.2 0.0 copy-start.2
  106.2 2.3 %copy.21 = bf16[256,2048]{1,0:T(8,128)(2,1)} copy(bf16[256,2048]{1,0:T(8,128)(2,1)} %get-tuple-element.10) | data formatting | bytes 2097152
  108.5 0.0 copy-done.2
  108.6 0.0 copy-start.1
  108.6 0.7 copy.22
  109.2 0.3 copy-done.1
  109.5 0.7 copy.23
  (2 shorter events, 0.0 us)
Async XLA Ops:
  0.6 4.6 %copy-start = (bf16[256,16,128]{2,1,0:T(8,128)(2,1)S(1)}, bf16[256,16,128]{2,1,0:T(8,128)(2,1)}, u32[]{:S(2)}) copy-start(bf16[256,16,128]{2,1,0:T(8,128)(2,1)} %param.8) | copy-start | bytes 3145732
  106.2 2.4 %copy-start.2 = (bf16[32,2048]{1,0:T(8,128)(2,1)S(1)}, bf16[32,2048]{1,0:T(8,128)(2,1)}, u32[]{:S(2)}) copy-start(bf16[32,2048]{1,0:T(8,128)(2,1)} %get-tuple-element.11) | copy-start | bytes 393220
  108.6 1.0 copy-start.1

commit v3 on v2

--- a/solution.py
+++ b/solution.py
@@ -121,6 +121,8 @@
     dq_out,
     dk_out,
     dv_out,
+    q_heads,
+    do_heads,
     kv_at,
     kcat,
     vcat,
@@ -133,6 +135,7 @@
     stage,
     arrived,
     row_sum,
+    crossing,
     kv_send,
     kv_recv,
     dq_send,
@@ -201,6 +204,16 @@
     for half in range(2):
         kv_at[mine[half]] = kv_ref[pl.ds(half * block_len, block_len), :]
 
+    chunk = 32
+
+    def by_head(step, c):
+        at = pl.ds(pl.multiple_of(step * chunk, chunk), chunk)
+        q_heads[:, at, :] = jnp.swapaxes(q_ref[at], 0, 1)
+        do_heads[:, at, :] = jnp.swapaxes(do_ref[at], 0, 1)
+        return c
+
+    lax.fori_loop(0, 2 * block_len // chunk, by_head, 0)
+
     def kv_wait(position):
         remote(
             kv_ref.at[pl.ds(0, block_len), :],
@@ -227,15 +240,93 @@
         def _():
             copy.start()
 
+    mirror = lax.rem(me + n // 2, n)
+    near = me // (n // 2)
+
+    def used_near(half, position):
+        hit = [
+            jnp.where(used(half * per_kv + e, position), 1, 0) for e in range(per_kv)
+        ]
+        return functools.reduce(jnp.maximum, hit) > 0
+
     def part_copy(g, e, b):
-        device = g * per_kv + e
-        return device, remote(
+        slot = lax.rem(me + jnp.where(g == near, 0, n // 2), n)
+        return remote(
             stage.at[g, b, :, pl.ds(pl.multiple_of(e * rows, rows), rows), :],
+            arrived.at[slot, b],
+            part_send.at[g * per_kv + e, b],
+            part_recv.at[slot, b],
+            near * per_kv + e,
+        )
+
+    def cross_copy(b):
+        return remote(
+            crossing.at[b],
             arrived.at[me, b],
-            part_send.at[device, b],
+            part_send.at[mirror, b],
             part_recv.at[me, b],
-            device,
-        )
+            mirror,
+        )
+
+    def part_wait(slot, b):
+        remote(
+            crossing.at[b],
+            arrived.at[slot, b],
+            part_send.at[slot, b],
+            part_recv.at[slot, b],
+            mirror,
+        ).wait_recv()
+
+    part_rows = pl.ds(pl.multiple_of(lax.rem(me, per_kv) * rows, rows), rows)
+
+    def add_own(g):
+        def own(b, c):
+            row_sum[b] = jnp.zeros(row_sum.shape[1:], f32)
+
+            @pl.when(used(me, b))
+            def _():
+                row_sum[b] = stage[g, b, :, part_rows, :].astype(f32)
+
+            return c
+
+        lax.fori_loop(0, blocks, own, 0)
+
+    def add_peers(shift):
+        def peer(step, carry):
+            source = near * per_kv + lax.rem(me + step, per_kv)
+            slot = lax.rem(source + shift, n)
+
+            def one(b, c):
+                @pl.when(used(source, b))
+                def _():
+                    part_wait(slot, b)
+                    row_sum[b] += arrived[slot, b].astype(f32)
+
+                return c
+
+            lax.fori_loop(0, blocks, one, 0)
+            return carry
+
+        lax.fori_loop(1, per_kv, peer, 0)
+
+    def cross():
+        add_own(1 - near)
+        add_peers(n // 2)
+
+        def pack(b, c):
+            crossing[b] = row_sum[b].astype(bf16)
+            return c
+
+        lax.fori_loop(0, blocks, pack, 0)
+
+        def go(b, c):
+            @pl.when(used_near(near, b))
+            def _():
+                cross_copy(b).start()
+
+            return c
+
+        lax.fori_loop(0, blocks, go, 0)
 
     def wanted(a, j):
         top = jnp.where(a == 0, mine[0], mine[1])
@@ -258,7 +349,14 @@
                 query_at = lax.broadcasted_iota(jnp.int32, (block_len, wide), 1) % block_len
                 bias[here, :] = jnp.where(key_at <= query_at, 0.0, -jnp.inf)
             else:
-                off = jnp.where(listed_ref[a, j] > 0, 0.0, -jnp.inf)
+                top = jnp.where(a == 0, mine[0], mine[1])
+                if j == slots - 1:
+                    target, real = jnp.int32(0), top > window
+                else:
+                    target, real = top - j, top >= j
+                hits = [jnp.where(listed_ref[a, e] == target, 1, 0) for e in range(slots)]
+                hit = jnp.where(real, functools.reduce(jnp.maximum, hits), 0)
+                off = jnp.where(hit > 0, 0.0, -jnp.inf)
                 bias[here, :] = jnp.full((block_len, wide), off, f32)
         dk_acc[...] = jnp.zeros_like(dk_acc)
         dv_acc[...] = jnp.zeros_like(dv_acc)
@@ -272,19 +370,10 @@
             first = g * group_size + 2 * i
 
             def two(ref):
-                return jnp.concatenate(
-                    [
-                        ref[
-                            query_rows,
-                            pl.ds(pl.multiple_of((first + e) * head_dim, head_dim), head_dim),
-                        ]
-                        for e in range(2)
-                    ],
-                    axis=0,
-                )
-
-            q2 = two(q_ref)
-            do2 = two(do_ref)
+                return ref[pl.ds(first, 2), query_rows, :].reshape(wide, head_dim)
+
+            q2 = two(q_heads)
+            do2 = two(do_heads)
             scores = dot(kcat[...], q2, NT) * scale + bias[...]
             grad_probs = dot(vcat[...], do2, NT)
             row_max = jnp.max(scores, axis=0, keepdims=True)
@@ -311,8 +400,7 @@
 
     def step_of(step, carry):
         phase, a = step // 2, lax.rem(step, 2)
-        far = 1 - me // (n // 2)
-        g = jnp.where(phase == 0, far, 1 - far)
+        g = jnp.where(phase == 0, 1 - near, near)
 
         def arrivals(position, c):
             low_part = (
@@ -333,6 +421,10 @@
         def _():
             total[...] = jnp.zeros_like(total)
 
+        @pl.when(step == 2 * kv_heads - 1)
+        def _():
+            cross()
+
         attend(g, a)
 
         @pl.when(a == 1)
@@ -348,11 +440,9 @@
 
             def send(b, c):
                 for e in range(per_kv):
-                    device, copy = part_copy(g, e, b)
-
-                    @pl.when(used(me, b) & (device != me))
+                    @pl.when(used(me, b) & (lax.rem(me, per_kv) != e))
                     def _():
-                        copy.start()
+                        part_copy(g, e, b).start()
 
                 return c
 
@@ -367,41 +457,18 @@
         at = pl.ds(pl.multiple_of(me * wide + a * block_len, block_len), block_len)
         dq_out[:, at] = dq_stage[a, own_rows, :]
 
-    own_g = me // per_kv
-    part_rows = pl.ds(pl.multiple_of(lax.rem(me, per_kv) * rows, rows), rows)
-
-    def own(b, c):
-        row_sum[b] = jnp.zeros(row_sum.shape[1:], f32)
-
-        @pl.when(used(me, b))
-        def _():
-            row_sum[b] = stage[own_g, b, :, part_rows, :].astype(f32)
+    add_own(near)
+    add_peers(0)
+
+    def crossed(b, c):
+        @pl.when(used_near(1 - near, b))
+        def _():
+            part_wait(mirror, b)
+            row_sum[b] += arrived[mirror, b].astype(f32)
 
         return c
 
-    lax.fori_loop(0, blocks, own, 0)
-
-    def gather(step, carry):
-        source = lax.rem(me + step, n)
-
-        def one(b, c):
-            @pl.when(used(source, b))
-            def _():
-                remote(
-                    stage.at[0, b, :, pl.ds(0, rows), :],
-                    arrived.at[source, b],
-                    part_send.at[source, b],
-                    part_recv.at[source, b],
-                    source,
-                ).wait_recv()
-                row_sum[b] += arrived[source, b].astype(f32)
-
-            return c
-
-        lax.fori_loop(0, blocks, one, 0)
-        return carry
-
-    lax.fori_loop(1, n, gather, 0)
+    lax.fori_loop(0, blocks, crossed, 0)
     for b in range(blocks):
         at = 2 * b if b < n else 2 * (blocks - 1 - b) + 1
         here = pl.ds(at * block_len, block_len)
@@ -424,24 +491,25 @@
             @pl.when(used(other, mine[half]))
             def _():
                 kv_copy(half, other).wait_send()
-
-        def sent(b, c):
-            @pl.when(used(me, b))
-            def _():
-                remote(
-                    stage.at[0, b, :, pl.ds(0, rows), :],
-                    arrived.at[me, b],
-                    part_send.at[other, b],
-                    part_recv.at[me, b],
-                    other,
-                ).wait_send()
-
-            return c
-
-        lax.fori_loop(0, blocks, sent, 0)
         return carry
 
     lax.fori_loop(1, n, finish_dq, 0)
+
+    def sent(b, c):
+        for e in range(per_kv):
+            for g in range(kv_heads):
+
+                @pl.when(used(me, b) & (lax.rem(me, per_kv) != e))
+                def _():
+                    part_copy(g, e, b).wait_send()
+
+        @pl.when(used_near(near, b))
+        def _():
+            cross_copy(b).wait_send()
+
+        return c
+
+    lax.fori_loop(0, blocks, sent, 0)
 
 
 def fused(queries, grad_out, kv, listed, sizes):
@@ -463,6 +531,8 @@
             jax.ShapeDtypeStruct((rows, n * tokens), bf16),
         ],
         scratch_shapes=[
+            pltpu.VMEM((kv_heads * group_size, tokens, head_dim), bf16),
+            pltpu.VMEM((kv_heads * group_size, tokens, head_dim), bf16),
             pltpu.VMEM((blocks, block_len, 2 * kv_heads * head_dim), bf16),
             pltpu.VMEM((keys, head_dim), bf16),
             pltpu.VMEM((keys, head_dim), bf16),
@@ -475,6 +545,7 @@
             pltpu.VMEM((kv_heads, blocks, 2, head_dim, block_len), bf16),
             pltpu.VMEM((n, blocks, 2, rows, block_len), bf16),
             pltpu.VMEM((blocks, 2, rows, block_len), f32),
+            pltpu.VMEM((blocks, 2, rows, block_len), bf16),
             dma((2, n)),
             dma((blocks,)),
             dma((2, n)),
@@ -520,9 +591,7 @@
     if dense and kv_heads == 2 and q_heads == 2 * n and n % 2 == 0:
         sizes = (n, block_len, head_dim, kv_heads, group_size, slots)
         return tuple(
-            fused(
-                queries.reshape(tokens, -1), grad_out.reshape(tokens, -1), kv, listed, sizes
-            )
+            fused(queries, grad_out, kv, key_blocks, sizes)
         )
     kv_all = lax.all_gather(kv, "seq", axis=0, tiled=True)
     keys = slots * block_len

time: 112 us -> 94.6 us (0.84); the launches traced: 110 us -> 94.2 us
  Pallas kernels: 97.9 us -> 87.8 us
  local copies, waits for them, and re-layouts: 8.12 us -> 4.95 us
  other arithmetic: 3.48 us -> 0.72 us
    pallas_call x1, Pallas kernels: 97.9 us -> 87.8 us  [fused(): pl.pallas_call(functools.partial(fused_kernel, sizes), in_specs=[pl.Block...]
    reshape x1 -> x0, local copies, waits for them, and re-layouts: 3.06 us -> none  [per_device(): grad_out.reshape(tokens, -1)]
    reduce_or x2 -> x0, other arithmetic: 1.76 us -> none  [the longest x1 0.89 us: per_device(): jnp.any(key_blocks[:, None, :] == near[:, :, None], axis=2) & (near >= 0)]
    unnamed x9 -> x7, local copies, waits for them, and re-layouts: 3.95 us -> 3.95 us
where the time goes in v3:
time: 94.6 us; the launch traced here: 94.2 us
  Pallas kernels  87.8 us (93%)
  local copies, waits for them, and re-layouts  4.95 us (5%)
    pallas_call x1, Pallas kernels, fused(): pl.pallas_call(functools.partial(fused_kernel, sizes), in_specs=[pl.Block...  87.8 us
    unnamed x7, local copies, waits for them, and re-layouts  3.95 us

profile of v3, /device:TPU:22, one launch (start us, length us, event | category | flops | bytes accessed | tf_op | source)
XLA Modules:
  0.0 94.2 jit_solution(17447201091063893679)
XLA Ops:
  0.6 1.0 %copy_bitcast_fusion = (bf16[256,256]{1,0:T(8,128)(2,1)S(1)}, bf16[256,256]{1,0:T(8,128)(2,1)S(1)}) fusion(bf16[32,8,2,128]{3,2,1,0:T(2,128)(2,1)} %bitcast.6, bf16[32,8,2,128]{3,2,1,0:T(2,128)(2,1)} %bitcast.7), kind=kLoop, calls=%fused_computation.1 | loop fusion | bytes 524288 | tf_op jit(solution)/shard_map/reshape | solution.py:573
  1.6 0.7 pad_maximum_fusion.kv_ref
  2.4 87.8 %attention_backward_exchange.1 = (bf16[256,2048]{1,0:T(8,128)(2,1)}, bf16[32,2048]{1,0:T(8,128)(2,1)}, bf16[32,2048]{1,0:T(8,128)(2,1)}) custom-call(s32[2,8]{1,0:T(2,128)} %listed_ref.1, bf16[256,16,128]{2,1,0:T(8,128)(2,1)} %q_ref.1, bf16[256,16,128]{2,1,0:T(8,128)(2,1)} %do_ref.1, bf16[256,512]{1,0:T(8,128)(2,1)} %pad_maximum_fusion.kv_ref), custom_call_target="tpu_custom_call" | custom-call | tf_op jit(solution)/shard_map/attention_backward_exchange/pallas_call | solution.py:524
  90.2 0.0 copy-start.1
  90.2 2.3 %copy.15 = bf16[256,2048]{1,0:T(8,128)(2,1)} copy(bf16[256,2048]{1,0:T(8,128)(2,1)} %get-tuple-element.8) | data formatting | bytes 2097152
  92.6 0.0 copy-done.1
  92.6 0.0 copy-start
  92.6 0.7 copy.16
  93.2 0.3 copy-done
  93.5 0.7 copy.17
Async XLA Ops:
  90.2 2.4 %copy-start.1 = (bf16[32,2048]{1,0:T(8,128)(2,1)S(1)}, bf16[32,2048]{1,0:T(8,128)(2,1)}, u32[]{:S(2)}) copy-start(bf16[32,2048]{1,0:T(8,128)(2,1)} %get-tuple-element.9) | copy-start | bytes 393220
  92.6 1.0 %copy-start = (bf16[32,2048]{1,0:T(8,128)(2,1)S(1)}, bf16[32,2048]{1,0:T(8,128)(2,1)}, u32[]{:S(2)}) copy-start(bf16[32,2048]{1,0:T(8,128)(2,1)} %get-tuple-element.10) | copy-start | bytes 393220

commit v4 on v3

--- a/solution.py
+++ b/solution.py
@@ -183,6 +183,17 @@
         )
     pl.semaphore_wait(barrier, n - 1)
 
+    mirror = lax.rem(me + n // 2, n)
+    near = me // (n // 2)
+
+    def used_near(half, position):
+        hit = [
+            jnp.where(used(half * per_kv + e, position), 1, 0) for e in range(per_kv)
+        ]
+        return functools.reduce(jnp.maximum, hit) > 0
+
+    owned = (mirror, blocks - 1 - mirror)
+
     def kv_copy(half, device):
         return remote(
             kv_ref.at[pl.ds(half * block_len, block_len), :],
@@ -192,27 +203,45 @@
             device,
         )
 
-    far_first = sorted(range(1, n), key=lambda step: -min(step, n - step))
+    def kv_forward(half, device):
+        return remote(
+            kv_at.at[owned[half]],
+            kv_at.at[owned[half]],
+            kv_send.at[half, lax.rem(device + n // 2, n)],
+            kv_recv.at[owned[half]],
+            device,
+        )
+
+    def peer_of(step):
+        return near * per_kv + lax.rem(me + step, per_kv)
+
     for half in range(2):
-        for step in far_first:
-            device = lax.rem(me + step, n)
-
-            @pl.when(used(device, mine[half]))
+
+        @pl.when(used_near(1 - near, mine[half]))
+        def _():
+            kv_copy(half, mirror).start()
+
+    for half in range(2):
+        for step in range(1, per_kv):
+
+            @pl.when(used(peer_of(step), mine[half]))
             def _():
-                kv_copy(half, device).start()
+                kv_copy(half, peer_of(step)).start()
 
     for half in range(2):
         kv_at[mine[half]] = kv_ref[pl.ds(half * block_len, block_len), :]
 
-    chunk = 32
-
-    def by_head(step, c):
-        at = pl.ds(pl.multiple_of(step * chunk, chunk), chunk)
-        q_heads[:, at, :] = jnp.swapaxes(q_ref[at], 0, 1)
-        do_heads[:, at, :] = jnp.swapaxes(do_ref[at], 0, 1)
-        return c
-
-    lax.fori_loop(0, 2 * block_len // chunk, by_head, 0)
+    def kv_pass():
+        for half in range(2):
+
+            @pl.when(used_near(near, owned[half]))
+            def _():
+                kv_wait(owned[half])
+                for step in range(1, per_kv):
+
+                    @pl.when(used(peer_of(step), owned[half]))
+                    def _():
+                        kv_forward(half, peer_of(step)).start()
 
     def kv_wait(position):
         remote(
@@ -223,6 +252,18 @@
             me,
         ).wait_recv()
 
+    kv_pass()
+
+    chunk = 32
+
+    def by_head(step, c):
+        at = pl.ds(pl.multiple_of(step * chunk, chunk), chunk)
+        q_heads[:, at, :] = jnp.swapaxes(q_ref[at], 0, 1)
+        do_heads[:, at, :] = jnp.swapaxes(do_ref[at], 0, 1)
+        return c
+
+    lax.fori_loop(0, 2 * block_len // chunk, by_head, 0)
+
     def dq_copy(g, a, i):
         device = g * per_kv + i
         return device, remote(
@@ -239,15 +280,6 @@
         @pl.when(device != me)
         def _():
             copy.start()
-
-    mirror = lax.rem(me + n // 2, n)
-    near = me // (n // 2)
-
-    def used_near(half, position):
-        hit = [
-            jnp.where(used(half * per_kv + e, position), 1, 0) for e in range(per_kv)
-        ]
-        return functools.reduce(jnp.maximum, hit) > 0
 
     def part_copy(g, e, b):
         slot = lax.rem(me + jnp.where(g == near, 0, n // 2), n)
@@ -408,6 +440,7 @@
             )
             due = jnp.where(a == 0, low_part, used(me, position) & jnp.logical_not(low_part))
             other = (position != mine[0]) & (position != mine[1])
+            other = other & (position != owned[0]) & (position != owned[1])
 
             @pl.when(due & other & (phase == 0))
             def _():
@@ -486,14 +519,25 @@
                 other,
             ).wait_recv()
             dq_copy(0, a, other)[1].wait_send()
-        for half in range(2):
-
-            @pl.when(used(other, mine[half]))
+        return carry
+
+    lax.fori_loop(1, n, finish_dq, 0)
+
+    for half in range(2):
+
+        @pl.when(used_near(1 - near, mine[half]))
+        def _():
+            kv_copy(half, mirror).wait_send()
+
+        for step in range(1, per_kv):
+
+            @pl.when(used(peer_of(step), mine[half]))
             def _():
-                kv_copy(half, other).wait_send()
-        return carry
-
-    lax.fori_loop(1, n, finish_dq, 0)
+                kv_copy(half, peer_of(step)).wait_send()
+
+            @pl.when(used_near(near, owned[half]) & used(peer_of(step), owned[half]))
+            def _():
+                kv_forward(half, peer_of(step)).wait_send()
 
     def sent(b, c):
         for e in range(per_kv):

time: 94.6 us -> 83.1 us (0.88)
  Pallas kernels: 87.8 us -> 76.6 us
    pallas_call x1, Pallas kernels: 87.8 us -> 76.6 us  [fused(): pl.pallas_call(functools.partial(fused_kernel, sizes), in_specs=[pl.Block...]
where the time goes in v4:
time: 83.1 us; the launch traced here: 82.9 us
  Pallas kernels  76.6 us (92%)
  local copies, waits for them, and re-layouts  4.95 us (6%)
    pallas_call x1, Pallas kernels, fused(): pl.pallas_call(functools.partial(fused_kernel, sizes), in_specs=[pl.Block...  76.6 us
    unnamed x7, local copies, waits for them, and re-layouts  3.95 us

profile of v4, /device:TPU:22, one launch (start us, length us, event | category | flops | bytes accessed | tf_op | source)
XLA Modules:
  0.0 82.9 jit_solution(13552721023644101450)
XLA Ops:
  0.6 1.0 %copy_bitcast_fusion = (bf16[256,256]{1,0:T(8,128)(2,1)S(1)}, bf16[256,256]{1,0:T(8,128)(2,1)S(1)}) fusion(bf16[32,8,2,128]{3,2,1,0:T(2,128)(2,1)} %bitcast.6, bf16[32,8,2,128]{3,2,1,0:T(2,128)(2,1)} %bitcast.7), kind=kLoop, calls=%fused_computation.1 | loop fusion | bytes 524288 | tf_op jit(solution)/shard_map/reshape | solution.py:617
  1.6 0.7 pad_maximum_fusion.kv_ref
  2.4 76.6 %attention_backward_exchange.1 = (bf16[256,2048]{1,0:T(8,128)(2,1)}, bf16[32,2048]{1,0:T(8,128)(2,1)}, bf16[32,2048]{1,0:T(8,128)(2,1)}) custom-call(s32[2,8]{1,0:T(2,128)} %listed_ref.1, bf16[256,16,128]{2,1,0:T(8,128)(2,1)} %q_ref.1, bf16[256,16,128]{2,1,0:T(8,128)(2,1)} %do_ref.1, bf16[256,512]{1,0:T(8,128)(2,1)} %pad_maximum_fusion.kv_ref), custom_call_target="tpu_custom_call" | custom-call | tf_op jit(solution)/shard_map/attention_backward_exchange/pallas_call | solution.py:568
  79.0 0.0 copy-start.1
  79.0 2.3 %copy.15 = bf16[256,2048]{1,0:T(8,128)(2,1)} copy(bf16[256,2048]{1,0:T(8,128)(2,1)} %get-tuple-element.8) | data formatting | bytes 2097152
  81.3 0.0 copy-done.1
  81.3 0.0 copy-start
  81.3 0.7 copy.16
  82.0 0.3 copy-done
  82.3 0.7 copy.17
Async XLA Ops:
  79.0 2.4 %copy-start.1 = (bf16[32,2048]{1,0:T(8,128)(2,1)S(1)}, bf16[32,2048]{1,0:T(8,128)(2,1)}, u32[]{:S(2)}) copy-start(bf16[32,2048]{1,0:T(8,128)(2,1)} %get-tuple-element.9) | copy-start | bytes 393220
  81.3 1.0 %copy-start = (bf16[32,2048]{1,0:T(8,128)(2,1)S(1)}, bf16[32,2048]{1,0:T(8,128)(2,1)}, u32[]{:S(2)}) copy-start(bf16[32,2048]{1,0:T(8,128)(2,1)} %get-tuple-element.10) | copy-start | bytes 393220

commit v5 on v4

--- a/solution.py
+++ b/solution.py
@@ -221,12 +221,15 @@
         def _():
             kv_copy(half, mirror).start()
 
-    for half in range(2):
+    def direct(half, now):
         for step in range(1, per_kv):
 
-            @pl.when(used(peer_of(step), mine[half]))
+            @pl.when(used(peer_of(step), mine[half]) & now)
             def _():
                 kv_copy(half, peer_of(step)).start()
+
+    direct(0, near >= 0)
+    direct(1, near == 0)
 
     for half in range(2):
         kv_at[mine[half]] = kv_ref[pl.ds(half * block_len, block_len), :]
@@ -252,8 +255,6 @@
             me,
         ).wait_recv()
 
-    kv_pass()
-
     chunk = 32
 
     def by_head(step, c):
@@ -263,6 +264,9 @@
         return c
 
     lax.fori_loop(0, 2 * block_len // chunk, by_head, 0)
+
+    kv_pass()
+    direct(1, near == 1)
 
     def dq_copy(g, a, i):
         device = g * per_kv + i

time: 83.1 us -> 80.2 us (0.965)
  Pallas kernels: 76.6 us -> 73.6 us
    pallas_call x1, Pallas kernels: 76.6 us -> 73.6 us  [fused(): pl.pallas_call(functools.partial(fused_kernel, sizes), in_specs=[pl.Block...]
where the time goes in v5:
time: 80.2 us; the launch traced here: 80 us
  Pallas kernels  73.6 us (92%)
  local copies, waits for them, and re-layouts  4.95 us (6%)
    pallas_call x1, Pallas kernels, fused(): pl.pallas_call(functools.partial(fused_kernel, sizes), in_specs=[pl.Block...  73.6 us
    unnamed x7, local copies, waits for them, and re-layouts  3.95 us

profile of v5, /device:TPU:22, one launch (start us, length us, event | category | flops | bytes accessed | tf_op | source)
XLA Modules:
  0.0 80.0 jit_solution(8775547313749417000)
XLA Ops:
  0.6 1.0 %copy_bitcast_fusion = (bf16[256,256]{1,0:T(8,128)(2,1)S(1)}, bf16[256,256]{1,0:T(8,128)(2,1)S(1)}) fusion(bf16[32,8,2,128]{3,2,1,0:T(2,128)(2,1)} %bitcast.6, bf16[32,8,2,128]{3,2,1,0:T(2,128)(2,1)} %bitcast.7), kind=kLoop, calls=%fused_computation.1 | loop fusion | bytes 524288 | tf_op jit(solution)/shard_map/reshape | solution.py:621
  1.6 0.7 pad_maximum_fusion.kv_ref
  2.4 73.6 %attention_backward_exchange.1 = (bf16[256,2048]{1,0:T(8,128)(2,1)}, bf16[32,2048]{1,0:T(8,128)(2,1)}, bf16[32,2048]{1,0:T(8,128)(2,1)}) custom-call(s32[2,8]{1,0:T(2,128)} %listed_ref.1, bf16[256,16,128]{2,1,0:T(8,128)(2,1)} %q_ref.1, bf16[256,16,128]{2,1,0:T(8,128)(2,1)} %do_ref.1, bf16[256,512]{1,0:T(8,128)(2,1)} %pad_maximum_fusion.kv_ref), custom_call_target="tpu_custom_call" | custom-call | tf_op jit(solution)/shard_map/attention_backward_exchange/pallas_call | solution.py:572
  76.0 0.0 copy-start.1
  76.0 2.3 %copy.15 = bf16[256,2048]{1,0:T(8,128)(2,1)} copy(bf16[256,2048]{1,0:T(8,128)(2,1)} %get-tuple-element.8) | data formatting | bytes 2097152
  78.4 0.0 copy-done.1
  78.4 0.0 copy-start
  78.4 0.7 copy.16
  79.0 0.3 copy-done
  79.3 0.7 copy.17
Async XLA Ops:
  76.0 2.4 %copy-start.1 = (bf16[32,2048]{1,0:T(8,128)(2,1)S(1)}, bf16[32,2048]{1,0:T(8,128)(2,1)}, u32[]{:S(2)}) copy-start(bf16[32,2048]{1,0:T(8,128)(2,1)} %get-tuple-element.9) | copy-start | bytes 393220
  78.4 1.0 %copy-start = (bf16[32,2048]{1,0:T(8,128)(2,1)S(1)}, bf16[32,2048]{1,0:T(8,128)(2,1)}, u32[]{:S(2)}) copy-start(bf16[32,2048]{1,0:T(8,128)(2,1)} %get-tuple-element.10) | copy-start | bytes 393220
